TPU v7x, 256 devices: a whole 4x4x8 slice. The times are simulated.
256 devices in a mesh: gx: 8 (over x_hi, y), gy: 16 (over z, core), gz: 2 (over x_lo).
Axes of the slice: x: 4 (x_hi: 2, x_lo: 2; x = x_hi * 2 + x_lo), y: 4, z: 8, core: 2. Of those that a mesh axis runs over, the one named last changes fastest.
Arguments:
- flow_vector_lowres: float32 [3, 4, 512, 1024], P(None, 'gz', 'gy', 'gx'), may hold values from -3 to 3
- heat_anomaly_lowres: float32 [4, 512, 1024], P('gz', 'gy', 'gx'), may hold values from -6 to 6
- salt_content_anomaly: float32 [8, 2048, 1024], P('gz', ('gx', 'gy')), may hold values from -6 to 6
Outputs:
- updated_velocity: float32 [3, 4, 512, 1024], P(None, 'gz', 'gy', 'gx')
- temperature_new: float32 [4, 512, 1024], P('gz', 'gy', 'gx')
- salinity_new: float32 [8, 2048, 1024], P('gz', ('gx', 'gy'))
All inputs are finite; a program needn't handle non-finite values.
Results may differ from a plain program's by a relative error of at most 0.00002.
Values sent between devices are 32-bit elements; how exact they have to be, the bound alone decides.
No kernel may reach another device: no remote copies, remote signals or barrier semaphores. Data moves between devices by JAX's collectives and lax.ppermute only.
A program may use at most 128 MiB of HBM per device.

v0:
```python
import jax
import jax.numpy as jnp
import numpy as np
from jax import lax
from jax.experimental import pallas as pl
from jax.experimental.pallas import tpu as pltpu
from jax.sharding import PartitionSpec as P

F32 = jnp.float32
BF16 = jnp.bfloat16
DT = 0.1
EVEN = (-0.0390625, 0.2734375, 0.8203125, -0.0546875)
ODD = (-0.0546875, 0.8203125, 0.2734375, -0.0390625)
KINDS = (0.2, 0.2, 0.2, 0.15)
NX = 512
NF = 1024


def refine_matrix():
    matrix = np.zeros((256, 256), np.float32)
    for n in range(256):
        i = 64 + n // 2
        for k in range(4):
            matrix[i + k - (2 if n % 2 == 0 else 1), n] = (EVEN if n % 2 == 0 else ODD)[k]
    return matrix


def restrict_matrix():
    matrix = np.zeros((256, 128), np.float32)
    for n in range(256):
        matrix[n, n // 2] = 0.125
    return matrix


REFINE = refine_matrix()
REFINE_SPLIT = np.concatenate([REFINE[:, 0::2], REFINE[:, 1::2]], axis=1)
RESTRICT = restrict_matrix()


def dot(a, b):
    return jnp.dot(a, b, preferred_element_type=F32)


def split(x):
    high = x.astype(BF16)
    return high, (x - high.astype(F32)).astype(BF16)


def row(x, s):
    n = x.shape[0]
    return x if s % n == 0 else pltpu.roll(x, (-s) % n, 0)


def iota(shape, axis):
    return lax.broadcasted_iota(jnp.int32, shape, axis)


def right(x):
    n = x.shape[1]
    return jnp.where(iota(x.shape, 1) == n - 1, 0.0, pltpu.roll(x, n - 1, 1))


def left(x):
    n = x.shape[1]
    return jnp.where(iota(x.shape, 1) == 0, 0.0, pltpu.roll(x, 1, 1))


def weigh(weights, terms):
    total = None
    for w, t in zip(weights, terms):
        if t is not None:
            total = w * t if total is None else total + w * t
    return total


def refine_rows(x, keep):
    m2, m1, p1, p2 = (row(x, s)[:keep] for s in (-2, -1, 1, 2))
    x = x[:keep]
    return weigh(EVEN, (m2, m1, x, p1)), weigh(ODD, (m1, x, p1, p2))


def turn_blocks(x):
    lane = iota((8, 128), 1)
    low = lane < 64
    even = (lane // 32) % 2 == 0
    y0 = jnp.where(low, x[0], pltpu.roll(x[2], 64, 1))
    y2 = jnp.where(low, pltpu.roll(x[0], 64, 1), x[2])
    y1 = jnp.where(low, x[1], pltpu.roll(x[3], 64, 1))
    y3 = jnp.where(low, pltpu.roll(x[1], 64, 1), x[3])
    out = []
    for a, b in ((y0, y1), (y2, y3)):
        out.append(jnp.where(even, a, pltpu.roll(b, 32, 1)))
        out.append(jnp.where(even, pltpu.roll(a, 96, 1), b))
    return out


def restrict(total, matrix):
    high, low = split(total)
    parts = []
    for b in range(4):
        window = slice(256 * b, 256 * b + 256)
        parts.append(dot(high[:, window], matrix) + dot(low[:, window], matrix))
    return jnp.concatenate(parts, axis=1)


def fine_columns(high, low, matrix_ref):
    parts = []
    for b in range(-1, 4):
        window = slice(max(128 * b, 0), min(128 * b + 256, NX))
        if b == -1:
            matrix = matrix_ref[128:256, :]
        elif b == 3:
            matrix = matrix_ref[0:128, :]
        else:
            matrix = matrix_ref[...]
        parts.append((b, window, matrix))
    return [dot(high[:, w], m) + dot(low[:, w], m) for _, w, m in parts]


def refined_rows(x, matrix_ref):
    high, low = split(x)
    parts = []
    parts.append((high[:, :128], low[:, :128], matrix_ref[128:256, 128:256]))
    for b in range(3):
        w = slice(128 * b, 128 * b + 256)
        parts.append((high[:, w], low[:, w], matrix_ref[...]))
    parts.append((high[:, 384:], low[:, 384:], matrix_ref[0:128, 0:128]))
    return jnp.concatenate([dot(h, m) + dot(l, m) for h, l, m in parts], axis=1)


def heat_mean(planes, keep, matrix_ref):
    high, low = split(jnp.concatenate(planes, axis=0))
    sums = []
    for t in fine_columns(high, low, matrix_ref):
        q = t * (1.0 + 0.5 * t)
        q = q[:, :128] + q[:, 128:]
        sums.append(sum(q[keep * j : keep * j + keep] for j in range(len(planes))))
    rolled = [pltpu.roll(s, 64, 1) for s in sums]
    low_half = iota((keep, 128), 1) < 64
    return 0.125 * jnp.concatenate(
        [jnp.where(low_half, rolled[c], rolled[c + 1]) for c in range(4)], axis=1
    )


def upwind(speed, positive, below, above):
    return speed * jnp.where(positive, below, above)


def gathered(c_ref, u_ref, d_ref, f, m):
    first = iota((8, NX), 0) < 4
    d = d_ref[2 * f + m // 2]
    u = u_ref[2 * f + m // 2]
    if m % 2 == 0:
        rim = jnp.where(first, d, pltpu.roll(u, 4, 0))
    else:
        rim = jnp.where(first, pltpu.roll(d, 4, 0), u)
    return jnp.concatenate([c_ref[f, m], rim], axis=0)


def wide(ref, tile, rows):
    return jnp.concatenate([ref[tile, rows, :], ref[tile + 1, rows, :]], axis=-1)


def pack_kernel(flow_ref, heat_ref, salt_ref, restrict_ref, a_ref, g_ref, mean_ref, plane_ref, strip):
    z = lax.axis_index("gz")
    for lv in range(2):
        block = jnp.concatenate([flow_ref[0, lv], flow_ref[1, lv], flow_ref[2, lv], heat_ref[lv]], axis=0)
        turned = block.T
        for j in range(16):
            piece = turned[8 * j : 8 * j + 8]
            a_ref[j, 0, lv] = piece
            a_ref[j, 1, lv] = piece
    for l in range(4):
        for c in range(8):
            strip[c, l] = salt_ref[l, :, 128 * c : 128 * c + 128]
    for l in range(4):
        for q in range(2):
            for c in range(8):
                plane_ref[l, q, :, 128 * c : 128 * c + 128] = strip[c, l, pl.ds(q, 8, stride=2), :]
    totals = []
    for m in range(2):
        totals.append(sum(plane_ref[2 * m + p, q] for p in range(2) for q in range(2)))
    means = restrict(jnp.concatenate(totals, axis=0), restrict_ref[...])
    for m in range(2):
        mean_ref[m] = means[8 * m : 8 * m + 8]
        g_ref[8 + m] = means[8 * m : 8 * m + 8]
    for near in range(2):
        level = jnp.where(z == 0, 3 - near, near)
        for q in range(2):
            plane = plane_ref[level, q]
            for h in range(2):
                g_ref[4 * near + 2 * q + h] = plane[:, 512 * h : 512 * h + 512]


def turn_kernel(d_ref, salt_ref, mean_ref, g_ref, c_ref, up_ref, down_ref):
    z = lax.axis_index("gz")
    for m in range(4):
        for b in range(4):
            tiles = turn_blocks([d_ref[4 * b + j, m] for j in range(4)])
            for f in range(4):
                c_ref[f, m, :, 128 * b : 128 * b + 128] = tiles[f]
        own = mean_ref[m % 2]
        other = g_ref[8 + m % 2]
        c_ref[4, m] = jnp.where(z == m // 2, own, other)
    first = iota((8, NX), 0) < 4
    for f in range(5):
        for p in range(2):
            a = c_ref[f, 2 * p]
            b = c_ref[f, 2 * p + 1]
            down_ref[2 * f + p] = jnp.where(first, a, pltpu.roll(b, 4, 0))
            up_ref[2 * f + p] = jnp.where(first, pltpu.roll(a, 4, 0), b)
    down_ref[12] = jnp.zeros((8, NX), F32)
    up_ref[12] = jnp.zeros((8, NX), F32)
    for h in range(2):
        w = slice(512 * h, 512 * h + 512)
        for l in range(4):
            down_ref[10 + h, 2 * l : 2 * l + 2, :] = salt_ref[l, 0:2, w]
            up_ref[10 + h, 2 * l : 2 * l + 2, :] = salt_ref[l, 14:16, w]
        down_ref[12, h : h + 1, :] = g_ref[h, 0:1, :]
        up_ref[12, h : h + 1, :] = g_ref[2 + h, 7:8, :]


def coarse_rate(q, below, above, speeds, positives, diffusion, keep):
    x = q[:keep]
    up = (above - x, right(x) - x, row(q, 1)[:keep] - x)
    down = (x - below, x - left(x), x - row(q, -1)[:keep])
    spread = (up[0] - down[0]) + (up[1] - down[1]) + (up[2] - down[2])
    carried = sum(upwind(a, s, d, u) for a, s, d, u in zip(speeds, positives, down, up))
    return diffusion * spread - carried


def salt_step(x, below, above, before, after, speeds):
    up = (above - x, after - x, right(x) - x)
    down = (x - below, x - before, x - left(x))
    spread = (up[0] - down[0]) + (up[1] - down[1]) + (up[2] - down[2])
    carried = sum(upwind(a, a > 0, d, u) for a, d, u in zip(speeds, down, up))
    return (DT * 0.05 / 0.25) * spread - (DT / 0.5) * carried


def coarse_kernel(
    c_ref, ur_ref, dr_ref, salt_ref, g_ref, refine_ref, refine_split_ref, restrict_ref,
    msg_ref, mid_out_ref, cp, mp, vel,
):
    z = lax.axis_index("gz")
    place = lax.axis_index("gx") * 16 + lax.axis_index("gy")
    zero = jnp.zeros((16, NX), F32)
    for f in range(4):
        for k in (0, 1, 6, 7):
            cp[f, k] = zero
            mp[f, k] = zero
        for m in range(4):
            cp[f, m + 2] = gathered(c_ref, ur_ref, dr_ref, f, m)
    for f in range(3):
        for m in range(2):
            for p in range(2):
                level = weigh(EVEN if p == 0 else ODD, [cp[f, 2 * z + m + p + k] for k in range(4)])
                even, odd = refine_rows(level, 8)
                vel[f, 2 * m + p] = refined_rows(jnp.concatenate([even, odd], axis=0), refine_ref)
    rows16 = iota((16, NX), 0)
    inside = ((rows16 < 8) | (rows16 >= 12) | (place != 127)) & ((rows16 < 12) | (place != 0))
    for m in range(4):
        planes = []
        for p in range(2):
            terms = [cp[3, m + p + k] if 2 <= m + p + k < 6 else None for k in range(4)]
            planes.extend(refine_rows(weigh(EVEN if p == 0 else ODD, terms), 16))
        buoyancy = heat_mean(planes, 16, refine_split_ref) - 0.8 * gathered(c_ref, ur_ref, dr_ref, 4, m)
        speeds = [cp[f, m + 2] for f in range(3)]
        positives = [s > 0 for s in speeds]
        for f in range(4):
            q = cp[f, m + 2]
            rate = coarse_rate(q, cp[f, m + 1], cp[f, m + 3], speeds, positives, KINDS[f], 16)
            if f == 0:
                rate = rate + buoyancy
            mid = jnp.where(inside, q + DT * rate, 0.0)
            mp[f, m + 2] = mid
            if f < 3:
                mid_out_ref[f, m] = mid
    line = iota((8, NF), 0)
    totals = []
    for m in range(2):
        total = None
        for p in range(2):
            l = 2 * m + p
            own = [salt_ref[l, q] for q in range(2)]
            following = jnp.where(line == 7, wide(dr_ref, 10, slice(2 * l, 2 * l + 1)), pltpu.roll(own[0], 7, 0))
            preceding = jnp.where(line == 0, wide(ur_ref, 10, slice(2 * l + 1, 2 * l + 2)), pltpu.roll(own[1], 1, 0))
            around = ((preceding, own[1]), (own[0], following))
            for q in range(2):
                near = wide(g_ref, 2 * q, slice(0, 8))
                if l == 0:
                    below = jnp.where(z == 1, near, 0.0)
                else:
                    below = salt_ref[l - 1, q]
                if l == 3:
                    above = jnp.where(z == 0, near, 0.0)
                else:
                    above = salt_ref[l + 1, q]
                speeds = [vel[f, l, 8 * q : 8 * q + 8, :] for f in (0, 2, 1)]
                x = own[q]
                mid = x + salt_step(x, below, above, around[q][0], around[q][1], speeds)
                total = mid if total is None else total + mid
        totals.append(total)
    means = restrict(jnp.concatenate(totals, axis=0), restrict_ref[...])
    for m in range(2):
        planes = []
        for p in range(2):
            level = weigh(EVEN if p == 0 else ODD, [mp[3, 2 * z + m + p + k] for k in range(4)])
            planes.extend(refine_rows(level, 8))
        buoyancy = heat_mean(planes, 8, refine_split_ref) - 0.8 * means[8 * m : 8 * m + 8]
        at = 2 * z + m + 2
        speeds = [mp[f, at, 0:8, :] for f in range(3)]
        positives = [s > 0 for s in speeds]
        ends = []
        for f in range(4):
            q = mp[f, at]
            rate = coarse_rate(q, mp[f, at - 1, 0:8, :], mp[f, at + 1, 0:8, :], speeds, positives, KINDS[f], 8)
            if f == 0:
                rate = rate + buoyancy
            ends.append(0.5 * cp[f, at, 0:8, :] + 0.5 * (q[:8] + DT * rate))
        for b in range(4):
            tiles = turn_blocks([ends[f][:, 128 * b : 128 * b + 128] for f in range(4)])
            for j in range(4):
                msg_ref[4 * b + j, m] = tiles[j]


def salt_kernel(
    c_ref, ur_ref, dr_ref, salt_ref, g_ref, mid_ref, refine_ref, out_ref, cp, ss, sm, vel, near_vel, mv, strip,
):
    z = lax.axis_index("gz")
    place = lax.axis_index("gx") * 16 + lax.axis_index("gy")
    zero = jnp.zeros((16, NX), F32)
    for f in range(3):
        for k in (0, 1, 6, 7):
            cp[f, k] = zero
            mv[f, k] = zero
        for m in range(4):
            cp[f, m + 2] = gathered(c_ref, ur_ref, dr_ref, f, m)
            mv[f, m + 2] = mid_ref[f, m]
    for f in range(3):
        for m in range(2):
            for p in range(2):
                level = weigh(EVEN if p == 0 else ODD, [cp[f, 2 * z + m + p + k] for k in range(4)])
                even, odd = refine_rows(level, 16)
                vel[f, 2 * m + p] = refined_rows(jnp.concatenate([even, odd], axis=0), refine_ref)
        weights = [jnp.where(z == 0, EVEN[k], ODD[k]) for k in range(4)]
        even, odd = refine_rows(weigh(weights, [cp[f, 2 + k] for k in range(4)]), 8)
        near_vel[f] = refined_rows(jnp.concatenate([even, odd], axis=0), refine_ref)
    line = iota((8, NF), 0)
    for q in range(2):
        for l in range(4):
            ss[q, l + 1, 0:8, :] = salt_ref[l, q]
            d = wide(dr_ref, 10, slice(2 * l + q, 2 * l + q + 1))
            u = wide(ur_ref, 10, slice(2 * l + q, 2 * l + q + 1))
            ss[q, l + 1, 8:16, :] = jnp.where(line == 0, d, jnp.where(line == 7, u, 0.0))
        near = wide(g_ref, 2 * q, slice(0, 8))
        if q == 0:
            edge = jnp.concatenate([dr_ref[12, 0:1, :], dr_ref[12, 1:2, :]], axis=-1)
            rim = jnp.where(line == 0, edge, 0.0)
        else:
            edge = jnp.concatenate([ur_ref[12, 0:1, :], ur_ref[12, 1:2, :]], axis=-1)
            rim = jnp.where(line == 7, edge, 0.0)
        whole = jnp.concatenate([near, rim], axis=0)
        ss[q, 0] = jnp.where(z == 1, whole, 0.0)
        ss[q, 5] = jnp.where(z == 0, whole, 0.0)
    line16 = iota((16, NF), 0)
    inside = ((line16 < 8) | (line16 >= 12) | (place != 127)) & ((line16 < 12) | (place != 0))
    for l in range(1, 5):
        pair = [ss[0, l], ss[1, l]]
        around = ((row(pair[1], -1), pair[1]), (pair[0], row(pair[0], 1)))
        for q in range(2):
            speeds = [vel[f, l - 1, 16 * q : 16 * q + 16, :] for f in (0, 2, 1)]
            x = pair[q]
            mid = x + salt_step(x, ss[q, l - 1], ss[q, l + 1], around[q][0], around[q][1], speeds)
            sm[q, l] = jnp.where(inside, mid, 0.0)
    pair = [jnp.where(z == 0, ss[q, 5], ss[q, 0]) for q in range(2)]
    around = ((row(pair[1], -1)[:8], pair[1][:8]), (pair[0][:8], row(pair[0], 1)[:8]))
    for q in range(2):
        far = wide(g_ref, 4 + 2 * q, slice(0, 8))
        below = jnp.where(z == 0, ss[q, 4, 0:8, :], far)
        above = jnp.where(z == 0, far, ss[q, 1, 0:8, :])
        speeds = [near_vel[f, 8 * q : 8 * q + 8, :] for f in (0, 2, 1)]
        x = pair[q][:8]
        mid = x + salt_step(x, below, above, around[q][0], around[q][1], speeds)
        sm[q, 0, 0:8, :] = jnp.where(z == 1, mid, 0.0)
        sm[q, 5, 0:8, :] = jnp.where(z == 0, mid, 0.0)
    for f in range(3):
        for m in range(2):
            for p in range(2):
                level = weigh(EVEN if p == 0 else ODD, [mv[f, 2 * z + m + p + k] for k in range(4)])
                even, odd = refine_rows(level, 8)
                vel[f, 2 * m + p, 0:16, :] = refined_rows(jnp.concatenate([even, odd], axis=0), refine_ref)
    for l in range(1, 5):
        pair = [sm[0, l], sm[1, l]]
        around = ((row(pair[1], -1)[:8], pair[1][:8]), (pair[0][:8], row(pair[0], 1)[:8]))
        for q in range(2):
            speeds = [vel[f, l - 1, 8 * q : 8 * q + 8, :] for f in (0, 2, 1)]
            x = pair[q][:8]
            step = salt_step(x, sm[q, l - 1, 0:8, :], sm[q, l + 1, 0:8, :], around[q][0], around[q][1], speeds)
            end = 0.5 * ss[q, l, 0:8, :] + 0.5 * (x + step)
            for c in range(8):
                strip[c, l - 1, pl.ds(q, 8, stride=2), :] = end[:, 128 * c : 128 * c + 128]
        for c in range(8):
            out_ref[l - 1, :, 128 * c : 128 * c + 128] = strip[c, l - 1]


def unpack_kernel(x_ref, flow_ref, heat_ref):
    for lv in range(2):
        turned = jnp.concatenate([x_ref[j, lv] for j in range(16)], axis=0).T
        for f in range(3):
            flow_ref[f, lv] = turned[32 * f : 32 * f + 32]
        heat_ref[lv] = turned[96:128]


def call(kernel, name, outs, scratch=(), limit=None):
    return pl.pallas_call(
        kernel,
        name=name,
        out_shape=[jax.ShapeDtypeStruct(s, F32) for s in outs],
        scratch_shapes=list(scratch),
    )


def on_device(flow, heat, salt):
    ring = 128
    up = [(i, i + 1) for i in range(ring - 1)]
    down = [(j, i) for i, j in up]
    refine = jnp.asarray(REFINE, BF16)
    refine_split = jnp.asarray(REFINE_SPLIT, BF16)
    restrict_m = jnp.asarray(RESTRICT, BF16)
    vmem = pltpu.VMEM
    a, g, means, planes = call(
        pack_kernel,
        "pack",
        [(16, 2, 2, 8, 128), (10, 8, NX), (2, 8, NX), (4, 2, 8, NF)],
        [vmem((8, 4, 16, 128), F32)],
    )(flow, heat, salt, restrict_m)
    g = lax.ppermute(g, "gz", [(0, 1), (1, 0)])
    d = lax.all_to_all(a.reshape(32, 2, 8, 128), ("gy", "gz"), 0, 0, tiled=True)
    c, u, w = call(turn_kernel, "turn", [(5, 4, 8, NX), (13, 8, NX), (13, 8, NX)])(
        d.reshape(16, 4, 8, 128), salt, means, g
    )
    u = lax.ppermute(u, ("gx", "gy"), up)
    w = lax.ppermute(w, ("gx", "gy"), down)
    msg, mid = call(
        coarse_kernel,
        "coarse",
        [(16, 2, 8, 128), (3, 4, 16, NX)],
        [vmem((4, 8, 16, NX), F32), vmem((4, 8, 16, NX), F32), vmem((3, 4, 16, NF), F32)],
    )(c, u, w, planes, g, refine, refine_split, restrict_m)
    back = lax.all_to_all(msg, "gy", 0, 0, tiled=True)
    (salt_end,) = call(
        salt_kernel,
        "salt",
        [(4, 16, NF)],
        [
            vmem((3, 8, 16, NX), F32),
            vmem((2, 6, 16, NF), F32),
            vmem((2, 6, 16, NF), F32),
            vmem((3, 4, 32, NF), F32),
            vmem((3, 16, NF), F32),
            vmem((3, 8, 16, NX), F32),
            vmem((8, 4, 16, 128), F32),
        ],
    )(c, u, w, planes, g, mid, refine)
    flow_end, heat_end = call(unpack_kernel, "unpack", [(3, 2, 32, 128), (2, 32, 128)])(back)
    return flow_end, heat_end, salt_end


def solution(mesh):
    specs = (P(None, "gz", "gy", "gx"), P("gz", "gy", "gx"), P("gz", ("gx", "gy"), None))
    return jax.shard_map(on_device, mesh=mesh, in_specs=specs, out_specs=specs, check_vma=False)
```

profile of v0, /device:TPU:25, one launch (start us, length us, event | category | flops | bytes accessed | tf_op | source)
XLA Modules:
  0.0 66.9 jit_solution(6028030152232527476)
XLA Ops:
  0.6 2.0 %pack.1 = (f32[16,2,2,8,128]{4,3,2,1,0:T(8,128)}, f32[10,8,512]{2,1,0:T(8,128)}, f32[2,8,512]{2,1,0:T(8,128)}, f32[4,2,8,1024]{3,2,1,0:T(8,128)}) custom-call(f32[3,2,32,128]{3,2,1,0:T(8,128)} %flow_ref.1, f32[2,32,128]{2,1,0:T(8,128)} %heat_ref.1, f32[4,16,1024]{2,1,0:T(8,128)} %salt_ref.3, bf16[256,128]{1,0:T(8,128)(2,1)} %constant.8.clone.restrict_ref), custom_call_target="tpu_custom_call" | custom-call | tf_op jit(solution)/shard_map/pack/pallas_call | solution.py:431
  2.6 0.0 copy-start.5
  2.6 10.4 %all-to-all-start = ((f32[32,2,8,128]{3,2,1,0:T(8,128)}), f32[32,2,8,128]{3,2,1,0:T(8,128)S(1)}, u32[]{:S(2)}, u32[]{:S(2)}) async-start(f32[32,2,8,128]{3,2,1,0:T(8,128)} %bitcast.3), calls=%async_computation | async-start | bytes 524288 | tf_op jit(solution)/shard_map/all_to_all | solution.py:438
  13.0 0.0 copy-done.5
  13.0 1.4 %collective-permute-start = (f32[10,8,512]{2,1,0:T(8,128)S(1)}, f32[10,8,512]{2,1,0:T(8,128)S(1)}, u32[]{:S(2)}, u32[]{:S(2)}) collective-permute-start(f32[10,8,512]{2,1,0:T(8,128)S(1)} %copy-done.5), channel_id=1, source_target_pairs={{0,1},{1,0},{2,3},{3,2},{4,5},{5,4},{6,7},{7,6},{8,9},{9,8},{10,11... | collective-permute-start | bytes 491528 | tf_op jit(solution)/shard_map/ppermute | solution.py:437
  14.4 5.6 %collective-permute-done.g_ref = f32[10,8,512]{2,1,0:T(8,128)S(1)} collective-permute-done((f32[10,8,512]{2,1,0:T(8,128)S(1)}, f32[10,8,512]{2,1,0:T(8,128)S(1)}, u32[]{:S(2)}, u32[]{:S(2)}) %collective-permute-start) | collective-permute-done | bytes 163872 | tf_op jit(solution)/shard_map/ppermute | solution.py:437
  20.0 0.0 copy-start
  20.0 4.4 %all-to-all-done = f32[32,2,8,128]{3,2,1,0:T(8,128)S(1)} async-done(((f32[32,2,8,128]{3,2,1,0:T(8,128)}), f32[32,2,8,128]{3,2,1,0:T(8,128)S(1)}, u32[]{:S(2)}, u32[]{:S(2)}) %all-to-all-start) | async-done | bytes 262176 | tf_op jit(solution)/shard_map/all_to_all | solution.py:438
  24.4 0.0 copy-start.1
  24.4 0.0 copy-done
  24.4 0.7 %copy-done.1 = f32[32,2,8,128]{3,2,1,0:T(8,128)} copy-done((f32[32,2,8,128]{3,2,1,0:T(8,128)}, f32[32,2,8,128]{3,2,1,0:T(8,128)S(1)}, u32[]{:S(2)}) %copy-start.1) | copy-done | bytes 262168
  25.1 2.2 %turn.1 = (f32[5,4,8,512]{3,2,1,0:T(8,128)}, f32[13,8,512]{2,1,0:T(8,128)}, f32[13,8,512]{2,1,0:T(8,128)}) custom-call(f32[16,4,8,128]{3,2,1,0:T(8,128)} %bitcast.2, f32[4,16,1024]{2,1,0:T(8,128)} %salt_ref.3, f32[2,8,512]{2,1,0:T(8,128)} %get-tuple-element.15.mean_ref, f32[10,8,512]{2,1,0:T(8,128)} %copy-done), custom_call_target="tpu_custom_call" | custom-call | tf_op jit(solution)/shard_map/turn/pallas_call | solution.py:439
  27.3 3.3 %collective-permute-start.1 = (f32[13,8,512]{2,1,0:T(8,128)}, f32[13,8,512]{2,1,0:T(8,128)S(1)}, u32[]{:S(2)}, u32[]{:S(2)}) collective-permute-start(f32[13,8,512]{2,1,0:T(8,128)} %get-tuple-element.18), channel_id=1, source_target_pairs={{0,2},{2,4},{4,6},{6,8},{8,10},{10,12},{12,14},{14,16},{16,18},{18... | collective-permute-start | bytes 638984 | tf_op jit(solution)/shard_map/ppermute | solution.py:442
  30.6 1.9 %collective-permute-start.2 = (f32[13,8,512]{2,1,0:T(8,128)}, f32[13,8,512]{2,1,0:T(8,128)S(1)}, u32[]{:S(2)}, u32[]{:S(2)}) collective-permute-start(f32[13,8,512]{2,1,0:T(8,128)} %get-tuple-element.19), channel_id=1, source_target_pairs={{2,0},{4,2},{6,4},{8,6},{10,8},{12,10},{14,12},{16,14},{18,16},{20... | collective-permute-start | bytes 638984 | tf_op jit(solution)/shard_map/ppermute | solution.py:443
  32.5 1.2 %collective-permute-done.1.ur_ref = f32[13,8,512]{2,1,0:T(8,128)S(1)} collective-permute-done((f32[13,8,512]{2,1,0:T(8,128)}, f32[13,8,512]{2,1,0:T(8,128)S(1)}, u32[]{:S(2)}, u32[]{:S(2)}) %collective-permute-start.1) | collective-permute-done | bytes 213024 | tf_op jit(solution)/shard_map/ppermute | solution.py:442
  33.7 0.0 copy-start.2
  33.7 4.3 %collective-permute-done.2.dr_ref = f32[13,8,512]{2,1,0:T(8,128)S(1)} collective-permute-done((f32[13,8,512]{2,1,0:T(8,128)}, f32[13,8,512]{2,1,0:T(8,128)S(1)}, u32[]{:S(2)}, u32[]{:S(2)}) %collective-permute-start.2) | collective-permute-done | bytes 213024 | tf_op jit(solution)/shard_map/ppermute | solution.py:443
  38.0 0.0 copy-start.3
  38.0 0.0 copy-done.2
  38.0 0.7 copy-done.3
  38.7 5.7 %coarse.1 = (f32[16,2,8,128]{3,2,1,0:T(8,128)}, f32[3,4,16,512]{3,2,1,0:T(8,128)}) custom-call(f32[5,4,8,512]{3,2,1,0:T(8,128)} %get-tuple-element.17.c_ref, f32[13,8,512]{2,1,0:T(8,128)} %copy-done.2, f32[13,8,512]{2,1,0:T(8,128)} %copy-done.3, f32[4,2,8,1024]{3,2,1,0:T(8,128)} %get-tuple-element.20.salt_ref, f32[10,8,512]{2,1,0:T(8,128)} %copy-done, ...), custom_call_target="tpu_custom_call" | custom-call | tf_op jit(solution)/shard_map/coarse/pallas_call | solution.py:444
  44.3 11.4 %all-to-all-start.1 = ((f32[16,2,8,128]{3,2,1,0:T(8,128)}), f32[16,2,8,128]{3,2,1,0:T(8,128)S(1)}, u32[]{:S(2)}, u32[]{:S(2)}) async-start(f32[16,2,8,128]{3,2,1,0:T(8,128)} %get-tuple-element.21), calls=%async_computation.1 | async-start | bytes 262144 | tf_op jit(solution)/shard_map/all_to_all | solution.py:450
  55.7 6.4 %salt.1 = f32[4,16,1024]{2,1,0:T(8,128)} custom-call(f32[5,4,8,512]{3,2,1,0:T(8,128)} %get-tuple-element.17.c_ref, f32[13,8,512]{2,1,0:T(8,128)} %copy-done.2, f32[13,8,512]{2,1,0:T(8,128)} %copy-done.3, f32[4,2,8,1024]{3,2,1,0:T(8,128)} %get-tuple-element.20.salt_ref, f32[10,8,512]{2,1,0:T(8,128)} %copy-done, f32[3,4,16,512]{3,2,1,0:T(8,128)} %get-tuple-element.24.mid_ref, ...), custom_call_target="tpu_custom_call" | custom-call | tf_op jit(solution)/shard_map/salt/pallas_call | solution.py:451
  62.1 2.5 %all-to-all-done.1.x_ref = f32[16,2,8,128]{3,2,1,0:T(8,128)S(1)} async-done(((f32[16,2,8,128]{3,2,1,0:T(8,128)}), f32[16,2,8,128]{3,2,1,0:T(8,128)S(1)}, u32[]{:S(2)}, u32[]{:S(2)}) %all-to-all-start.1) | async-done | bytes 131104 | tf_op jit(solution)/shard_map/all_to_all | solution.py:450
  64.6 0.0 copy-start.4
  64.6 0.7 copy-done.4
  65.3 1.6 %unpack.1 = (f32[3,2,32,128]{3,2,1,0:T(8,128)}, f32[2,32,128]{2,1,0:T(8,128)}) custom-call(f32[16,2,8,128]{3,2,1,0:T(8,128)} %copy-done.4), custom_call_target="tpu_custom_call" | custom-call | tf_op jit(solution)/shard_map/unpack/pallas_call | solution.py:465
Async XLA Ops:
  2.6 10.4 %copy-start.5 = (f32[10,8,512]{2,1,0:T(8,128)S(1)}, f32[10,8,512]{2,1,0:T(8,128)}, u32[]{:S(2)}) copy-start(f32[10,8,512]{2,1,0:T(8,128)} %get-tuple-element.16) | copy-start | bytes 491524
  2.6 21.8 %all-to-all-start = ((f32[32,2,8,128]{3,2,1,0:T(8,128)}), f32[32,2,8,128]{3,2,1,0:T(8,128)S(1)}, u32[]{:S(2)}, u32[]{:S(2)}) async-start(f32[32,2,8,128]{3,2,1,0:T(8,128)} %bitcast.3), calls=%async_computation | async-start | bytes 524288 | tf_op jit(solution)/shard_map/all_to_all | solution.py:438
  13.0 7.0 %collective-permute-start = (f32[10,8,512]{2,1,0:T(8,128)S(1)}, f32[10,8,512]{2,1,0:T(8,128)S(1)}, u32[]{:S(2)}, u32[]{:S(2)}) collective-permute-start(f32[10,8,512]{2,1,0:T(8,128)S(1)} %copy-done.5), channel_id=1, source_target_pairs={{0,1},{1,0},{2,3},{3,2},{4,5},{5,4},{6,7},{7,6},{8,9},{9,8},{10,11... | collective-permute-start | bytes 491528 | tf_op jit(solution)/shard_map/ppermute | solution.py:437
  20.0 4.4 %copy-start = (f32[10,8,512]{2,1,0:T(8,128)}, f32[10,8,512]{2,1,0:T(8,128)S(1)}, u32[]{:S(2)}) copy-start(f32[10,8,512]{2,1,0:T(8,128)S(1)} %collective-permute-done.g_ref) | copy-start | bytes 491524
  24.4 0.7 %copy-start.1 = (f32[32,2,8,128]{3,2,1,0:T(8,128)}, f32[32,2,8,128]{3,2,1,0:T(8,128)S(1)}, u32[]{:S(2)}) copy-start(f32[32,2,8,128]{3,2,1,0:T(8,128)S(1)} %all-to-all-done) | copy-start | bytes 786436
  27.3 6.4 %collective-permute-start.1 = (f32[13,8,512]{2,1,0:T(8,128)}, f32[13,8,512]{2,1,0:T(8,128)S(1)}, u32[]{:S(2)}, u32[]{:S(2)}) collective-permute-start(f32[13,8,512]{2,1,0:T(8,128)} %get-tuple-element.18), channel_id=1, source_target_pairs={{0,2},{2,4},{4,6},{6,8},{8,10},{10,12},{12,14},{14,16},{16,18},{18... | collective-permute-start | bytes 638984 | tf_op jit(solution)/shard_map/ppermute | solution.py:442
  30.6 7.4 %collective-permute-start.2 = (f32[13,8,512]{2,1,0:T(8,128)}, f32[13,8,512]{2,1,0:T(8,128)S(1)}, u32[]{:S(2)}, u32[]{:S(2)}) collective-permute-start(f32[13,8,512]{2,1,0:T(8,128)} %get-tuple-element.19), channel_id=1, source_target_pairs={{2,0},{4,2},{6,4},{8,6},{10,8},{12,10},{14,12},{16,14},{18,16},{20... | collective-permute-start | bytes 638984 | tf_op jit(solution)/shard_map/ppermute | solution.py:443
  33.7 4.3 %copy-start.2 = (f32[13,8,512]{2,1,0:T(8,128)}, f32[13,8,512]{2,1,0:T(8,128)S(1)}, u32[]{:S(2)}) copy-start(f32[13,8,512]{2,1,0:T(8,128)S(1)} %collective-permute-done.1.ur_ref) | copy-start | bytes 638980
  38.0 0.7 %copy-start.3 = (f32[13,8,512]{2,1,0:T(8,128)}, f32[13,8,512]{2,1,0:T(8,128)S(1)}, u32[]{:S(2)}) copy-start(f32[13,8,512]{2,1,0:T(8,128)S(1)} %collective-permute-done.2.dr_ref) | copy-start | bytes 638980
  44.3 20.3 %all-to-all-start.1 = ((f32[16,2,8,128]{3,2,1,0:T(8,128)}), f32[16,2,8,128]{3,2,1,0:T(8,128)S(1)}, u32[]{:S(2)}, u32[]{:S(2)}) async-start(f32[16,2,8,128]{3,2,1,0:T(8,128)} %get-tuple-element.21), calls=%async_computation.1 | async-start | bytes 262144 | tf_op jit(solution)/shard_map/all_to_all | solution.py:450
  64.6 0.7 copy-start.4
where the time goes:
time: 67.3 us; the launch traced here: 66.9 us
  starting transfers between devices  28.4 us (42%)
  Pallas kernels  17.9 us (27%)
  waiting for transfers between devices  17.9 us (27%)
  local copies, waits for them, and re-layouts  2.04 us (3%)
    all_to_all x1, starting transfers between devices, on_device(): back = lax.all_to_all(msg, 'gy', 0, 0, tiled=True)  11.4 us
    all_to_all x1, starting transfers between devices, on_device(): d = lax.all_to_all(a.reshape(32, 2, 8, 128), ('gy', 'gz'), 0, 0, tiled=True)  10.4 us
    pallas_call x1, Pallas kernels, on_device(): call(salt_kernel, 'salt', [(4, 16, NF)], [vmem((3, 8, 16, NX), F32), vmem...  6.36 us
    pallas_call x1, Pallas kernels, on_device(): call(coarse_kernel, 'coarse', [(16, 2, 8, 128), (3, 4, 16, NX)], [vmem((4...  5.66 us
    ppermute x1, waiting for transfers between devices, on_device(): g = lax.ppermute(g, 'gz', [(0, 1), (1, 0)])  5.58 us
    all_to_all x1, waiting for transfers between devices, on_device(): d = lax.all_to_all(a.reshape(32, 2, 8, 128), ('gy', 'gz'), 0, 0, tiled=True)  4.4 us
    ppermute x1, waiting for transfers between devices, on_device(): w = lax.ppermute(w, ('gx', 'gy'), down)  4.29 us
    ppermute x1, starting transfers between devices, on_device(): u = lax.ppermute(u, ('gx', 'gy'), up)  3.28 us
  transfers between devices with their start and end apart: 5, of which 5 were waited for; matrix products, arithmetic and copies ran while one was open for 0% of the time, Pallas kernels for 10%

commit v1 on v0

v1 whole, which is shorter than its diff:
```python
import jax
import jax.numpy as jnp
import numpy as np
from jax import lax
from jax.experimental import pallas as pl
from jax.experimental.pallas import tpu as pltpu
from jax.sharding import PartitionSpec as P

F32 = jnp.float32
BF16 = jnp.bfloat16
DT = 0.1
EVEN = (-0.0390625, 0.2734375, 0.8203125, -0.0546875)
ODD = (-0.0546875, 0.8203125, 0.2734375, -0.0390625)
KINDS = (0.2, 0.2, 0.2, 0.15)
NX = 512
NF = 1024


def refine_matrix():
    matrix = np.zeros((256, 256), np.float32)
    for n in range(256):
        i = 64 + n // 2
        for k in range(4):
            matrix[i + k - (2 if n % 2 == 0 else 1), n] = (EVEN if n % 2 == 0 else ODD)[k]
    return matrix


def restrict_matrix():
    matrix = np.zeros((256, 128), np.float32)
    for n in range(256):
        matrix[n, n // 2] = 0.125
    return matrix


REFINE = refine_matrix()
REFINE_SPLIT = np.concatenate([REFINE[:, 0::2], REFINE[:, 1::2]], axis=1)
RESTRICT = restrict_matrix()


def dot(a, b):
    return jnp.dot(a, b, preferred_element_type=F32)


def split(x):
    high = x.astype(BF16)
    return high, (x - high.astype(F32)).astype(BF16)


def row(x, s):
    n = x.shape[0]
    return x if s % n == 0 else pltpu.roll(x, (-s) % n, 0)


def iota(shape, axis):
    return lax.broadcasted_iota(jnp.int32, shape, axis)


def right(x):
    n = x.shape[1]
    return jnp.where(iota(x.shape, 1) == n - 1, 0.0, pltpu.roll(x, n - 1, 1))


def left(x):
    n = x.shape[1]
    return jnp.where(iota(x.shape, 1) == 0, 0.0, pltpu.roll(x, 1, 1))


def weigh(weights, terms):
    total = None
    for w, t in zip(weights, terms):
        if t is not None:
            total = w * t if total is None else total + w * t
    return total


def refine_rows(x, keep):
    m2, m1, p1, p2 = (row(x, s)[:keep] for s in (-2, -1, 1, 2))
    x = x[:keep]
    return weigh(EVEN, (m2, m1, x, p1)), weigh(ODD, (m1, x, p1, p2))


def turn_blocks(x):
    lane = iota((8, 128), 1)
    low = lane < 64
    even = (lane // 32) % 2 == 0
    y0 = jnp.where(low, x[0], pltpu.roll(x[2], 64, 1))
    y2 = jnp.where(low, pltpu.roll(x[0], 64, 1), x[2])
    y1 = jnp.where(low, x[1], pltpu.roll(x[3], 64, 1))
    y3 = jnp.where(low, pltpu.roll(x[1], 64, 1), x[3])
    out = []
    for a, b in ((y0, y1), (y2, y3)):
        out.append(jnp.where(even, a, pltpu.roll(b, 32, 1)))
        out.append(jnp.where(even, pltpu.roll(a, 96, 1), b))
    return out


def restrict(total, matrix):
    high, low = split(total)
    parts = []
    for b in range(4):
        window = slice(256 * b, 256 * b + 256)
        parts.append(dot(high[:, window], matrix) + dot(low[:, window], matrix))
    return jnp.concatenate(parts, axis=1)


def fine_columns(high, low, matrix_ref):
    parts = []
    for b in range(-1, 4):
        window = slice(max(128 * b, 0), min(128 * b + 256, NX))
        if b == -1:
            matrix = matrix_ref[128:256, :]
        elif b == 3:
            matrix = matrix_ref[0:128, :]
        else:
            matrix = matrix_ref[...]
        parts.append((b, window, matrix))
    return [dot(high[:, w], m) + dot(low[:, w], m) for _, w, m in parts]


def refined_rows(x, matrix_ref):
    high, low = split(x)
    parts = []
    parts.append((high[:, :128], low[:, :128], matrix_ref[128:256, 128:256]))
    for b in range(3):
        w = slice(128 * b, 128 * b + 256)
        parts.append((high[:, w], low[:, w], matrix_ref[...]))
    parts.append((high[:, 384:], low[:, 384:], matrix_ref[0:128, 0:128]))
    return jnp.concatenate([dot(h, m) + dot(l, m) for h, l, m in parts], axis=1)


def heat_mean(planes, keep, matrix_ref):
    high, low = split(jnp.concatenate(planes, axis=0))
    sums = []
    for t in fine_columns(high, low, matrix_ref):
        q = t * (1.0 + 0.5 * t)
        q = q[:, :128] + q[:, 128:]
        sums.append(sum(q[keep * j : keep * j + keep] for j in range(len(planes))))
    rolled = [pltpu.roll(s, 64, 1) for s in sums]
    low_half = iota((keep, 128), 1) < 64
    return 0.125 * jnp.concatenate(
        [jnp.where(low_half, rolled[c], rolled[c + 1]) for c in range(4)], axis=1
    )


def upwind(speed, positive, below, above):
    return speed * jnp.where(positive, below, above)


def wide(ref, tile, rows):
    return jnp.concatenate([ref[tile, rows, :], ref[tile + 1, rows, :]], axis=-1)


def pack_kernel(flow_hbm, heat_hbm, salt_hbm, restrict_hbm, a_ref, g_ref, mean_ref, plane_ref,
                tile, strip, restrict_ref, sems):
    z = lax.axis_index("gz")
    flow_in = [pltpu.make_async_copy(flow_hbm, tile.at[pl.ds(0, 3)], sems.at[0])]
    flow_in.append(pltpu.make_async_copy(heat_hbm, tile.at[3], sems.at[1]))
    salt_in = [
        pltpu.make_async_copy(salt_hbm.at[:, :, pl.ds(128 * c, 128)], strip.at[c], sems.at[3 + c]) for c in range(8)
    ]
    salt_in.append(pltpu.make_async_copy(restrict_hbm, restrict_ref, sems.at[2]))
    for copy in flow_in + salt_in:
        copy.start()
    for copy in flow_in:
        copy.wait()
    for lv in range(2):
        turned = jnp.concatenate([tile[f, lv] for f in range(4)], axis=0).T
        for j in range(16):
            piece = turned[8 * j : 8 * j + 8]
            a_ref[j, 0, lv] = piece
            a_ref[j, 1, lv] = piece
    for copy in salt_in:
        copy.wait()
    for l in range(4):
        for q in range(2):
            for c in range(8):
                plane_ref[l, q, :, 128 * c : 128 * c + 128] = strip[c, l, pl.ds(q, 8, stride=2), :]
    totals = []
    for m in range(2):
        totals.append(sum(plane_ref[2 * m + p, q] for p in range(2) for q in range(2)))
    means = restrict(jnp.concatenate(totals, axis=0), restrict_ref[...])
    for m in range(2):
        mean_ref[m] = means[8 * m : 8 * m + 8]
        g_ref[8 + m] = means[8 * m : 8 * m + 8]
    for near in range(2):
        level = jnp.where(z == 0, 3 - near, near)
        for q in range(2):
            plane = plane_ref[level, q]
            for h in range(2):
                g_ref[4 * near + 2 * q + h] = plane[:, 512 * h : 512 * h + 512]


def mean_of(mean_ref, g_ref, z, m):
    return jnp.where(z == m // 2, mean_ref[m % 2], g_ref[8 + m % 2])


def send_kernel(d_ref, plane_ref, mean_ref, g_ref, c_ref, near_ref, far_ref, up_ref, down_ref):
    z = lax.axis_index("gz")
    leads = lax.rem(lax.axis_index("gy"), 2) == 0
    for m in range(4):
        for b in range(4):
            tiles = turn_blocks([d_ref[4 * b + j, m] for j in range(4)])
            for f in range(4):
                c_ref[f, m, :, 128 * b : 128 * b + 128] = tiles[f]
        c_ref[4, m] = mean_of(mean_ref, g_ref, z, m)
    first = iota((8, NX), 0) < 4
    for f in range(5):
        for p in range(2):
            a = c_ref[f, 2 * p]
            b = c_ref[f, 2 * p + 1]
            down_ref[2 * f + p] = jnp.where(first, a, pltpu.roll(b, 4, 0))
            up_ref[2 * f + p] = jnp.where(first, pltpu.roll(a, 4, 0), b)
    down_ref[12] = jnp.zeros((8, NX), F32)
    up_ref[12] = jnp.zeros((8, NX), F32)
    for h in range(2):
        w = slice(512 * h, 512 * h + 512)
        for l in range(4):
            for q in range(2):
                k = 2 * l + q
                down_ref[10 + h, k : k + 1, :] = plane_ref[l, q, 0:1, w]
                up_ref[10 + h, k : k + 1, :] = plane_ref[l, q, 7:8, w]
        down_ref[12, h : h + 1, :] = g_ref[h, 0:1, :]
        up_ref[12, h : h + 1, :] = g_ref[2 + h, 7:8, :]
    for t in range(13):
        up = up_ref[t]
        down = down_ref[t]
        near_ref[t] = jnp.where(leads, up, down)
        far_ref[t] = jnp.where(leads, down, up)


def coarse_rate(q, below, above, speeds, positives, diffusion, keep):
    x = q[:keep]
    up = (above - x, right(x) - x, row(q, 1)[:keep] - x)
    down = (x - below, x - left(x), x - row(q, -1)[:keep])
    spread = (up[0] - down[0]) + (up[1] - down[1]) + (up[2] - down[2])
    carried = sum(upwind(a, s, d, u) for a, s, d, u in zip(speeds, positives, down, up))
    return diffusion * spread - carried


def salt_step(x, below, above, before, after, speeds):
    up = (above - x, after - x, right(x) - x)
    down = (x - below, x - before, x - left(x))
    spread = (up[0] - down[0]) + (up[1] - down[1]) + (up[2] - down[2])
    carried = sum(upwind(a, a > 0, d, u) for a, d, u in zip(speeds, down, up))
    return (DT * 0.05 / 0.25) * spread - (DT / 0.5) * carried


def edge_row(ref, k):
    whole = jnp.concatenate([ref[10, k : k + 1, :], ref[11, k : k + 1, :]], axis=-1)
    return jnp.broadcast_to(whole, (8, NF))


def near_edge(ref):
    whole = jnp.concatenate([ref[12, 0:1, :], ref[12, 1:2, :]], axis=-1)
    return jnp.broadcast_to(whole, (8, NF))


def levels_of(fields, f, start, parity):
    return weigh(EVEN if parity == 0 else ODD, [fields[f, start + parity + k] for k in range(4)])


def rim_of(ur_ref, dr_ref, f, m):
    first = iota((8, NX), 0) < 4
    d = dr_ref[2 * f + m // 2]
    u = ur_ref[2 * f + m // 2]
    if m % 2 == 0:
        return jnp.where(first, d, pltpu.roll(u, 4, 0))
    return jnp.where(first, pltpu.roll(d, 4, 0), u)


def coarse_kernel(
    c_ref, near_ref, far_ref, plane_ref, g_ref, refine_ref, refine_split_ref, restrict_ref,
    msg_ref, cp, mp, salt_mid, ur_ref, dr_ref, vel,
):
    z = lax.axis_index("gz")
    leads = lax.rem(lax.axis_index("gy"), 2) == 0
    place = lax.axis_index("gx") * 16 + lax.axis_index("gy")
    for t in range(13):
        near = near_ref[t]
        far = far_ref[t]
        ur_ref[t] = jnp.where(leads, far, near)
        dr_ref[t] = jnp.where(leads, near, far)
    zero = jnp.zeros((16, NX), F32)
    for f in range(4):
        for k in (0, 1, 6, 7):
            cp[f, k] = zero
            mp[f, k] = zero
        for m in range(4):
            cp[f, m + 2, 0:8, :] = c_ref[f, m]
            cp[f, m + 2, 8:16, :] = rim_of(ur_ref, dr_ref, f, m)
    for f in range(3):
        for m in range(2):
            for p in range(2):
                even, odd = refine_rows(levels_of(cp, f, 2 * z + m, p), 8)
                vel[f, 2 * m + p] = refined_rows(jnp.concatenate([even, odd], axis=0), refine_ref)
    rows16 = iota((16, NX), 0)
    inside = ((rows16 < 8) | (rows16 >= 12) | (place != 127)) & ((rows16 < 12) | (place != 0))
    for m in range(4):
        planes = []
        for p in range(2):
            terms = [cp[3, m + p + k] if 2 <= m + p + k < 6 else None for k in range(4)]
            planes.extend(refine_rows(weigh(EVEN if p == 0 else ODD, terms), 16))
        salt_mean = jnp.concatenate([c_ref[4, m], rim_of(ur_ref, dr_ref, 4, m)], axis=0)
        buoyancy = heat_mean(planes, 16, refine_split_ref) - 0.8 * salt_mean
        speeds = [cp[f, m + 2] for f in range(3)]
        positives = [s > 0 for s in speeds]
        for f in range(4):
            q = cp[f, m + 2]
            rate = coarse_rate(q, cp[f, m + 1], cp[f, m + 3], speeds, positives, KINDS[f], 16)
            if f == 0:
                rate = rate + buoyancy
            mp[f, m + 2] = jnp.where(inside, q + DT * rate, 0.0)
    line = iota((8, NF), 0)
    totals = []
    for m in range(2):
        total = None
        for p in range(2):
            l = 2 * m + p
            own = [plane_ref[l, q] for q in range(2)]
            following = jnp.where(line == 7, edge_row(dr_ref, 2 * l), pltpu.roll(own[0], 7, 0))
            preceding = jnp.where(line == 0, edge_row(ur_ref, 2 * l + 1), pltpu.roll(own[1], 1, 0))
            around = ((preceding, own[1]), (own[0], following))
            for q in range(2):
                near = wide(g_ref, 2 * q, slice(0, 8))
                below = jnp.where(z == 1, near, 0.0) if l == 0 else plane_ref[l - 1, q]
                above = jnp.where(z == 0, near, 0.0) if l == 3 else plane_ref[l + 1, q]
                speeds = [vel[f, l, 8 * q : 8 * q + 8, :] for f in (0, 2, 1)]
                x = own[q]
                mid = x + salt_step(x, below, above, around[q][0], around[q][1], speeds)
                salt_mid[l, q] = mid
                total = mid if total is None else total + mid
        totals.append(total)
    means = restrict(jnp.concatenate(totals, axis=0), restrict_ref[...])
    for m in range(2):
        planes = []
        for p in range(2):
            planes.extend(refine_rows(levels_of(mp, 3, 2 * z + m, p), 8))
        buoyancy = heat_mean(planes, 8, refine_split_ref) - 0.8 * means[8 * m : 8 * m + 8]
        at = 2 * z + m + 2
        speeds = [mp[f, at, 0:8, :] for f in range(3)]
        positives = [s > 0 for s in speeds]
        ends = []
        for f in range(4):
            q = mp[f, at]
            rate = coarse_rate(q, mp[f, at - 1, 0:8, :], mp[f, at + 1, 0:8, :], speeds, positives, KINDS[f], 8)
            if f == 0:
                rate = rate + buoyancy
            ends.append(0.5 * cp[f, at, 0:8, :] + 0.5 * (q[:8] + DT * rate))
        for b in range(4):
            tiles = turn_blocks([ends[f][:, 128 * b : 128 * b + 128] for f in range(4)])
            for j in range(4):
                msg_ref[4 * b + j, m] = tiles[j]


def salt_kernel(
    cp, mv, salt_mid_ref, plane_ref, ur_ref, dr_ref, g_ref, refine_ref, out_ref, vel, near_vel, strip,
):
    z = lax.axis_index("gz")
    place = lax.axis_index("gx") * 16 + lax.axis_index("gy")
    top = iota((8, NX), 0) == 0
    for f in range(3):
        rims = []
        for m in range(2):
            for p in range(2):
                even, odd = refine_rows(levels_of(cp, f, 2 * z + m, p), 16)
                rims.append(jnp.where(top, even[8:], odd[8:]))
        weights = [jnp.where(z == 0, EVEN[k], ODD[k]) for k in range(4)]
        rims.extend(refine_rows(weigh(weights, [cp[f, 2 + k] for k in range(4)]), 8))
        near_vel[f] = refined_rows(jnp.concatenate(rims, axis=0), refine_ref)
    for f in range(3):
        for m in range(2):
            for p in range(2):
                even, odd = refine_rows(levels_of(mv, f, 2 * z + m, p), 8)
                vel[f, 2 * m + p] = refined_rows(jnp.concatenate([even, odd], axis=0), refine_ref)
    line = iota((8, NF), 0)
    rim = [jnp.where(line == 0, edge_row(dr_ref, 2 * l), edge_row(ur_ref, 2 * l + 1)) for l in range(4)]
    near_rim = jnp.where(line == 0, near_edge(dr_ref), near_edge(ur_ref))
    bottom = jnp.where(z == 1, near_rim, 0.0)
    roof = jnp.where(z == 0, near_rim, 0.0)
    alive = ((line != 0) | (place != 127)) & ((line != 7) | (place != 0))
    rim_mid = []
    for l in range(4):
        before = jnp.where(line == 0, pltpu.roll(plane_ref[l, 1], 1, 0), edge_row(ur_ref, 2 * l))
        after = jnp.where(line == 0, edge_row(dr_ref, 2 * l + 1), pltpu.roll(plane_ref[l, 0], 7, 0))
        speeds = [near_vel[f, 8 * l : 8 * l + 8, :] for f in (0, 2, 1)]
        below = bottom if l == 0 else rim[l - 1]
        above = roof if l == 3 else rim[l + 1]
        mid = rim[l] + salt_step(rim[l], below, above, before, after, speeds)
        rim_mid.append(jnp.where(alive, mid, 0.0))
    near = [wide(g_ref, 2 * q, slice(0, 8)) for q in range(2)]
    before = jnp.where(line == 0, near_edge(ur_ref), pltpu.roll(near[1], 1, 0))
    after = jnp.where(line == 7, near_edge(dr_ref), pltpu.roll(near[0], 7, 0))
    around = ((before, near[1]), (near[0], after))
    near_mid = []
    for q in range(2):
        far = wide(g_ref, 4 + 2 * q, slice(0, 8))
        below = jnp.where(z == 0, plane_ref[3, q], far)
        above = jnp.where(z == 0, far, plane_ref[0, q])
        speeds = [near_vel[f, 32 + 8 * q : 40 + 8 * q, :] for f in (0, 2, 1)]
        near_mid.append(near[q] + salt_step(near[q], below, above, around[q][0], around[q][1], speeds))
    for l in range(4):
        pair = [salt_mid_ref[l, q] for q in range(2)]
        before = pltpu.roll(jnp.where(line == 7, rim_mid[l], pair[1]), 1, 0)
        after = pltpu.roll(jnp.where(line == 0, rim_mid[l], pair[0]), 7, 0)
        around = ((before, pair[1]), (pair[0], after))
        for q in range(2):
            speeds = [vel[f, l, 8 * q : 8 * q + 8, :] for f in (0, 2, 1)]
            below = jnp.where(z == 1, near_mid[q], 0.0) if l == 0 else salt_mid_ref[l - 1, q]
            above = jnp.where(z == 0, near_mid[q], 0.0) if l == 3 else salt_mid_ref[l + 1, q]
            x = pair[q]
            step = salt_step(x, below, above, around[q][0], around[q][1], speeds)
            end = 0.5 * plane_ref[l, q] + 0.5 * (x + step)
            for c in range(8):
                strip[c, l, pl.ds(q, 8, stride=2), :] = end[:, 128 * c : 128 * c + 128]
        for c in range(8):
            out_ref[l, :, 128 * c : 128 * c + 128] = strip[c, l]


def unpack_kernel(x_ref, flow_ref, heat_ref):
    for lv in range(2):
        turned = jnp.concatenate([x_ref[j, lv] for j in range(16)], axis=0).T
        for f in range(3):
            flow_ref[f, lv] = turned[32 * f : 32 * f + 32]
        heat_ref[lv] = turned[96:128]


SPACES = {"h": pl.BlockSpec(memory_space=pltpu.HBM), "v": pl.BlockSpec(memory_space=pltpu.VMEM)}


def call(kernel, name, ins, outs, scratch=()):
    return pl.pallas_call(
        kernel,
        name=name,
        in_specs=[SPACES[letter] for letter in ins],
        out_specs=[SPACES["v"] for _ in outs],
        out_shape=[jax.ShapeDtypeStruct(s, F32) for s in outs],
        scratch_shapes=list(scratch),
        compiler_params=pltpu.CompilerParams(vmem_limit_bytes=16 * 2**20),
    )


def swap(x, axes, n, start):
    pairs = []
    for i in range(start, n - 1, 2):
        pairs += [(i, i + 1), (i + 1, i)]
    return lax.ppermute(x, axes, pairs)


def on_device(flow, heat, salt):
    vmem = pltpu.VMEM
    refine = jnp.asarray(REFINE, BF16)
    refine_split = jnp.asarray(REFINE_SPLIT, BF16)
    restrict_m = jnp.asarray(RESTRICT, BF16)
    a, g, means, planes = call(
        pack_kernel,
        "pack",
        "hhhh",
        [(16, 2, 2, 8, 128), (10, 8, NX), (2, 8, NX), (4, 2, 8, NF)],
        [
            vmem((4, 2, 32, 128), F32),
            vmem((8, 4, 16, 128), F32),
            vmem((256, 128), BF16),
            pltpu.SemaphoreType.DMA((11,)),
        ],
    )(flow, heat, salt, restrict_m)
    g = swap(g, "gz", 2, 0)
    d = lax.all_to_all(a.reshape(32, 2, 8, 128), ("gy", "gz"), 0, 0, tiled=True)
    rims = [(13, 8, NX)] * 2
    c, near, far, _, _ = call(send_kernel, "send", "vvvv", [(5, 4, 8, NX)] + rims + rims)(
        d.reshape(16, 4, 8, 128), planes, means, g
    )
    near = swap(near, ("gx", "gy"), 128, 0)
    far = swap(far, ("gx", "gy"), 128, 1)
    fields = [(4, 8, 16, NX)] * 2
    msg, cp, mp, salt_mid, u, v = call(
        coarse_kernel,
        "coarse",
        "vvvvvvvv",
        [(16, 2, 8, 128)] + fields + [(4, 2, 8, NF)] + rims,
        [vmem((3, 4, 16, NF), F32)],
    )(c, near, far, planes, g, refine, refine_split, restrict_m)
    back = lax.all_to_all(msg, "gy", 0, 0, tiled=True)
    (salt_end,) = call(
        salt_kernel,
        "salt",
        "vvvvvvvv",
        [(4, 16, NF)],
        [vmem((3, 4, 16, NF), F32), vmem((3, 48, NF), F32), vmem((8, 4, 16, 128), F32)],
    )(cp, mp, salt_mid, planes, u, v, g, refine)
    flow_end, heat_end = call(unpack_kernel, "unpack", "v", [(3, 2, 32, 128), (2, 32, 128)])(back)
    return flow_end, heat_end, salt_end


def solution(mesh):
    specs = (P(None, "gz", "gy", "gx"), P("gz", "gy", "gx"), P("gz", ("gx", "gy"), None))
    return jax.shard_map(on_device, mesh=mesh, in_specs=specs, out_specs=specs, check_vma=False)
```

time: 67.3 us -> 59.9 us (0.89)
  the two profiles are of different devices: /device:TPU:25 before, /device:TPU:7 now
where the time goes in v1:
time: 59.9 us; the launch traced here: 59.5 us
  starting transfers between devices  23.3 us (39%)
  waiting for transfers between devices  21.8 us (36%)
  Pallas kernels  9.59 us (16%)
  local copies, waits for them, and re-layouts  4.12 us (7%)
  between operations  0.69 us (1%)
    ppermute x3, waiting for transfers between devices, swap(): return lax.ppermute(x, axes, pairs)  12 us
    all_to_all x1, starting transfers between devices, on_device(): d = lax.all_to_all(a.reshape(32, 2, 8, 128), ('gy', 'gz'), 0, 0, tiled=True)  10.4 us
    all_to_all x1, starting transfers between devices, on_device(): back = lax.all_to_all(msg, 'gy', 0, 0, tiled=True)  9.02 us
    all_to_all x1, waiting for transfers between devices, on_device(): back = lax.all_to_all(msg, 'gy', 0, 0, tiled=True)  6.13 us
    unnamed x16, local copies, waits for them, and re-layouts  4.12 us
    ppermute x3, starting transfers between devices, swap(): return lax.ppermute(x, axes, pairs)  3.88 us
    all_to_all x1, waiting for transfers between devices, on_device(): d = lax.all_to_all(a.reshape(32, 2, 8, 128), ('gy', 'gz'), 0, 0, tiled=True)  3.69 us
    pallas_call x1, Pallas kernels, on_device(): call(coarse_kernel, 'coarse', 'vvvvvvvv', [(16, 2, 8, 128)] + fields + [(...  3.5 us
  transfers between devices with their start and end apart: 5, of which 4 were waited for; matrix products, arithmetic and copies ran while one was open for 0% of the time, Pallas kernels for 5%

profile of v1, /device:TPU:7, one launch (start us, length us, event | category | flops | bytes accessed | tf_op | source)
XLA Modules:
  0.0 59.5 jit_solution(5144400884993336080)
XLA Ops:
  0.6 0.0 copy-start.1
  0.6 0.8 %copy-done.1 = bf16[256,128]{1,0:T(8,128)(2,1)S(1)} copy-done((bf16[256,128]{1,0:T(8,128)(2,1)S(1)}, bf16[256,128]{1,0:T(8,128)(2,1)}, u32[]{:S(2)}) %copy-start.1) | copy-done | bytes 65560
  1.5 0.0 copy-start.3
  1.5 0.9 %copy-done.3 = f32[4,16,1024]{2,1,0:T(8,128)S(1)} copy-done((f32[4,16,1024]{2,1,0:T(8,128)S(1)}, f32[4,16,1024]{2,1,0:T(8,128)}, u32[]{:S(2)}) %copy-start.3) | copy-done | bytes 262168
  2.4 0.0 copy-start.6
  2.4 0.9 %copy-done.6 = f32[3,2,32,128]{3,2,1,0:T(8,128)S(1)} copy-done((f32[3,2,32,128]{3,2,1,0:T(8,128)S(1)}, f32[3,2,32,128]{3,2,1,0:T(8,128)}, u32[]{:S(2)}) %copy-start.6) | copy-done | bytes 98328
  3.3 0.0 copy-start.7
  3.3 0.8 %copy-done.7 = f32[2,32,128]{2,1,0:T(8,128)S(1)} copy-done((f32[2,32,128]{2,1,0:T(8,128)S(1)}, f32[2,32,128]{2,1,0:T(8,128)}, u32[]{:S(2)}) %copy-start.7) | copy-done | bytes 32792
  4.1 1.3 %pack.1 = (f32[16,2,2,8,128]{4,3,2,1,0:T(8,128)}, f32[10,8,512]{2,1,0:T(8,128)S(1)}, f32[2,8,512]{2,1,0:T(8,128)S(1)}, f32[4,2,8,1024]{3,2,1,0:T(8,128)S(1)}) custom-call(f32[3,2,32,128]{3,2,1,0:T(8,128)S(1)} %copy-done.6, f32[2,32,128]{2,1,0:T(8,128)S(1)} %copy-done.7, f32[4,16,1024]{2,1,0:T(8,128)S(1)} %copy-done.3, bf16[256,128]{1,0:T(8,128)(2,1)S(1)} %copy-done.1), custom_call_target="tpu_custom_call" | custom-call | tf_op jit(solution)/shard_map/pack/pallas_call | solution.py:454
  5.3 10.4 %all-to-all-start = ((f32[32,2,8,128]{3,2,1,0:T(8,128)}), f32[32,2,8,128]{3,2,1,0:T(8,128)S(1)}, u32[]{:S(2)}, u32[]{:S(2)}) async-start(f32[32,2,8,128]{3,2,1,0:T(8,128)} %bitcast), calls=%async_computation | async-start | bytes 524288 | tf_op jit(solution)/shard_map/all_to_all | solution.py:467
  15.7 0.2 collective-permute-start
  15.9 7.0 %collective-permute-done.g_ref = f32[10,8,512]{2,1,0:T(8,128)S(1)} collective-permute-done((f32[10,8,512]{2,1,0:T(8,128)S(1)}, f32[10,8,512]{2,1,0:T(8,128)S(1)}, u32[]{:S(2)}, u32[]{:S(2)}) %collective-permute-start) | collective-permute-done | bytes 163872 | tf_op jit(solution)/shard_map/ppermute | solution.py:446
  22.9 3.7 %all-to-all-done = f32[32,2,8,128]{3,2,1,0:T(8,128)S(1)} async-done(((f32[32,2,8,128]{3,2,1,0:T(8,128)}), f32[32,2,8,128]{3,2,1,0:T(8,128)S(1)}, u32[]{:S(2)}, u32[]{:S(2)}) %all-to-all-start) | async-done | bytes 262176 | tf_op jit(solution)/shard_map/all_to_all | solution.py:467
  26.6 0.0 copy-start
  26.6 0.0 copy-start.2
  26.6 0.0 copy-start.4
  26.6 1.0 %send.1 = (f32[5,4,8,512]{3,2,1,0:T(8,128)S(1)}, f32[13,8,512]{2,1,0:T(8,128)S(1)}, f32[13,8,512]{2,1,0:T(8,128)S(1)}, f32[13,8,512]{2,1,0:T(8,128)}, f32[13,8,512]{2,1,0:T(8,128)}) custom-call(f32[16,4,8,128]{3,2,1,0:T(8,128)S(1)} %bitcast.2, f32[4,2,8,1024]{3,2,1,0:T(8,128)S(1)} %get-tuple-element.19.plane_ref, ...), custom_call_target="tpu_custom_call" | custom-call | tf_op jit(solution)/shard_map/send/pallas_call | solution.py:469
  27.6 1.6 %collective-permute-start.1 = (f32[13,8,512]{2,1,0:T(8,128)S(1)}, f32[13,8,512]{2,1,0:T(8,128)S(1)}, u32[]{:S(2)}, u32[]{:S(2)}) collective-permute-start(f32[13,8,512]{2,1,0:T(8,128)S(1)} %get-tuple-element.23), channel_id=1, source_target_pairs={{0,2},{2,0},{4,6},{6,4},{8,10},{10,8},{12,14},{14,12},{16,18},{18,... | collective-permute-start | bytes 638984 | tf_op jit(solution)/shard_map/ppermute | solution.py:446
  29.2 2.1 %collective-permute-start.2 = (f32[13,8,512]{2,1,0:T(8,128)S(1)}, f32[13,8,512]{2,1,0:T(8,128)S(1)}, u32[]{:S(2)}, u32[]{:S(2)}) collective-permute-start(f32[13,8,512]{2,1,0:T(8,128)S(1)} %get-tuple-element.24), channel_id=1, source_target_pairs={{2,4},{4,2},{6,8},{8,6},{10,12},{12,10},{14,16},{16,14},{18,20},{2... | collective-permute-start | bytes 638984 | tf_op jit(solution)/shard_map/ppermute | solution.py:446
  31.3 0.0 collective-permute-done.1.near_ref
  31.3 5.0 %collective-permute-done.2.far_ref = f32[13,8,512]{2,1,0:T(8,128)S(1)} collective-permute-done((f32[13,8,512]{2,1,0:T(8,128)S(1)}, f32[13,8,512]{2,1,0:T(8,128)S(1)}, u32[]{:S(2)}, u32[]{:S(2)}) %collective-permute-start.2) | collective-permute-done | bytes 213024 | tf_op jit(solution)/shard_map/ppermute | solution.py:446
  36.4 0.0 copy-done
  36.4 0.0 copy-done.2
  36.4 0.0 copy-done.4
  36.4 3.5 %coarse.1 = (f32[16,2,8,128]{3,2,1,0:T(8,128)S(1)}, f32[4,8,16,512]{3,2,1,0:T(8,128)S(1)}, f32[4,8,16,512]{3,2,1,0:T(8,128)S(1)}, f32[4,2,8,1024]{3,2,1,0:T(8,12...) custom-call(f32[5,4,8,512]{3,2,1,0:T(8,128)S(1)} %get-tuple-element.22.c_ref, ...), custom_call_target="tpu_custom_call" | custom-call | tf_op jit(solution)/shard_map/coarse/pallas_call | solution.py:475
  39.9 0.0 copy-start.5
  39.9 0.7 %copy-done.5 = f32[16,2,8,128]{3,2,1,0:T(8,128)} copy-done((f32[16,2,8,128]{3,2,1,0:T(8,128)}, f32[16,2,8,128]{3,2,1,0:T(8,128)S(1)}, u32[]{:S(2)}) %copy-start.5) | copy-done | bytes 131096
  40.6 9.0 %all-to-all-start.1 = ((f32[16,2,8,128]{3,2,1,0:T(8,128)}), f32[16,2,8,128]{3,2,1,0:T(8,128)S(1)}, u32[]{:S(2)}, u32[]{:S(2)}) async-start(f32[16,2,8,128]{3,2,1,0:T(8,128)} %copy-done.5), calls=%async_computation.1 | async-start | bytes 262144 | tf_op jit(solution)/shard_map/all_to_all | solution.py:482
  49.6 3.1 %salt.1 = f32[4,16,1024]{2,1,0:T(8,128)} custom-call(f32[4,8,16,512]{3,2,1,0:T(8,128)S(1)} %get-tuple-element.28.cp, f32[4,8,16,512]{3,2,1,0:T(8,128)S(1)} %get-tuple-element.29.mv, f32[4,2,8,1024]{3,2,1,0:T(8,128)S(1)} %get-tuple-element.30.salt_mid_ref, f32[4,2,8,1024]{3,2,1,0:T(8,128)S(1)} %get-tuple-element.19.plane_ref, ...), custom_call_target="tpu_custom_call" | custom-call | tf_op jit(solution)/shard_map/salt/pallas_call | solution.py:483
  52.6 6.1 %all-to-all-done.1.x_ref = f32[16,2,8,128]{3,2,1,0:T(8,128)S(1)} async-done(((f32[16,2,8,128]{3,2,1,0:T(8,128)}), f32[16,2,8,128]{3,2,1,0:T(8,128)S(1)}, u32[]{:S(2)}, u32[]{:S(2)}) %all-to-all-start.1) | async-done | bytes 131104 | tf_op jit(solution)/shard_map/all_to_all | solution.py:482
  58.8 0.7 %unpack.1 = (f32[3,2,32,128]{3,2,1,0:T(8,128)}, f32[2,32,128]{2,1,0:T(8,128)}) custom-call(f32[16,2,8,128]{3,2,1,0:T(8,128)S(1)} %all-to-all-done.1.x_ref), custom_call_target="tpu_custom_call" | custom-call | tf_op jit(solution)/shard_map/unpack/pallas_call | solution.py:490
Async XLA Ops:
  0.6 0.8 %copy-start.1 = (bf16[256,128]{1,0:T(8,128)(2,1)S(1)}, bf16[256,128]{1,0:T(8,128)(2,1)}, u32[]{:S(2)}) copy-start(bf16[256,128]{1,0:T(8,128)(2,1)} %constant.8.clone.restrict_hbm.restrict_ref) | copy-start | bytes 196612
  1.5 0.9 %copy-start.3 = (f32[4,16,1024]{2,1,0:T(8,128)S(1)}, f32[4,16,1024]{2,1,0:T(8,128)}, u32[]{:S(2)}) copy-start(f32[4,16,1024]{2,1,0:T(8,128)} %salt_hbm.1) | copy-start | bytes 786436
  2.4 0.9 %copy-start.6 = (f32[3,2,32,128]{3,2,1,0:T(8,128)S(1)}, f32[3,2,32,128]{3,2,1,0:T(8,128)}, u32[]{:S(2)}) copy-start(f32[3,2,32,128]{3,2,1,0:T(8,128)} %flow_hbm.1) | copy-start | bytes 294916
  3.3 0.8 %copy-start.7 = (f32[2,32,128]{2,1,0:T(8,128)S(1)}, f32[2,32,128]{2,1,0:T(8,128)}, u32[]{:S(2)}) copy-start(f32[2,32,128]{2,1,0:T(8,128)} %heat_hbm.1) | copy-start | bytes 98308
  5.3 21.3 %all-to-all-start = ((f32[32,2,8,128]{3,2,1,0:T(8,128)}), f32[32,2,8,128]{3,2,1,0:T(8,128)S(1)}, u32[]{:S(2)}, u32[]{:S(2)}) async-start(f32[32,2,8,128]{3,2,1,0:T(8,128)} %bitcast), calls=%async_computation | async-start | bytes 524288 | tf_op jit(solution)/shard_map/all_to_all | solution.py:467
  15.7 7.2 %collective-permute-start = (f32[10,8,512]{2,1,0:T(8,128)S(1)}, f32[10,8,512]{2,1,0:T(8,128)S(1)}, u32[]{:S(2)}, u32[]{:S(2)}) collective-permute-start(f32[10,8,512]{2,1,0:T(8,128)S(1)} %get-tuple-element.21), channel_id=1, source_target_pairs={{0,1},{1,0},{2,3},{3,2},{4,5},{5,4},{6,7},{7,6},{8,9},{9,8},{10,11... | collective-permute-start | bytes 491528 | tf_op jit(solution)/shard_map/ppermute | solution.py:446
  26.6 9.8 %copy-start = (bf16[256,256]{1,0:T(8,128)(2,1)S(1)}, bf16[256,256]{1,0:T(8,128)(2,1)}, u32[]{:S(2)}) copy-start(bf16[256,256]{1,0:T(8,128)(2,1)} %constant.6.clone.refine_ref) | copy-start | bytes 393220
  26.6 9.8 %copy-start.2 = (bf16[256,128]{1,0:T(8,128)(2,1)S(1)}, bf16[256,128]{1,0:T(8,128)(2,1)}, u32[]{:S(2)}) copy-start(bf16[256,128]{1,0:T(8,128)(2,1)} %constant.8.clone.restrict_hbm.restrict_ref) | copy-start | bytes 196612
  26.6 9.8 %copy-start.4 = (bf16[256,256]{1,0:T(8,128)(2,1)S(1)}, bf16[256,256]{1,0:T(8,128)(2,1)}, u32[]{:S(2)}) copy-start(bf16[256,256]{1,0:T(8,128)(2,1)} %constant.7.clone.refine_split_ref) | copy-start | bytes 393220
  27.6 3.7 %collective-permute-start.1 = (f32[13,8,512]{2,1,0:T(8,128)S(1)}, f32[13,8,512]{2,1,0:T(8,128)S(1)}, u32[]{:S(2)}, u32[]{:S(2)}) collective-permute-start(f32[13,8,512]{2,1,0:T(8,128)S(1)} %get-tuple-element.23), channel_id=1, source_target_pairs={{0,2},{2,0},{4,6},{6,4},{8,10},{10,8},{12,14},{14,12},{16,18},{18,... | collective-permute-start | bytes 638984 | tf_op jit(solution)/shard_map/ppermute | solution.py:446
  29.2 7.2 %collective-permute-start.2 = (f32[13,8,512]{2,1,0:T(8,128)S(1)}, f32[13,8,512]{2,1,0:T(8,128)S(1)}, u32[]{:S(2)}, u32[]{:S(2)}) collective-permute-start(f32[13,8,512]{2,1,0:T(8,128)S(1)} %get-tuple-element.24), channel_id=1, source_target_pairs={{2,4},{4,2},{6,8},{8,6},{10,12},{12,10},{14,16},{16,14},{18,20},{2... | collective-permute-start | bytes 638984 | tf_op jit(solution)/shard_map/ppermute | solution.py:446
  39.9 0.7 %copy-start.5 = (f32[16,2,8,128]{3,2,1,0:T(8,128)}, f32[16,2,8,128]{3,2,1,0:T(8,128)S(1)}, u32[]{:S(2)}) copy-start(f32[16,2,8,128]{3,2,1,0:T(8,128)S(1)} %get-tuple-element.25) | copy-start | bytes 393220
  40.6 18.2 %all-to-all-start.1 = ((f32[16,2,8,128]{3,2,1,0:T(8,128)}), f32[16,2,8,128]{3,2,1,0:T(8,128)S(1)}, u32[]{:S(2)}, u32[]{:S(2)}) async-start(f32[16,2,8,128]{3,2,1,0:T(8,128)} %copy-done.5), calls=%async_computation.1 | async-start | bytes 262144 | tf_op jit(solution)/shard_map/all_to_all | solution.py:482

commit v2 on v1

--- a/solution.py
+++ b/solution.py
@@ -32,9 +32,28 @@
     return matrix
 
 
+def level_row_matrix(levels, parts):
+    rows = np.zeros((2, 16, 16), np.float64)
+    for q, weights in enumerate((EVEN, ODD)):
+        for i in range(16):
+            for k in range(4):
+                rows[q, i, (i + k - 2 + q) % 16] = weights[k]
+    deep = np.zeros((len(levels), 4), np.float64)
+    for n, l in enumerate(levels):
+        for k in range(4):
+            m = l // 2 + k - 2 + l % 2
+            if 0 <= m < 4:
+                deep[n, m] = (EVEN, ODD)[l % 2][k]
+    whole = np.einsum("lm,qij->lqimj", deep, rows[:, :parts]).reshape(len(levels) * 2 * parts, 64)
+    high = whole.astype(np.float32).astype(jnp.bfloat16).astype(np.float64)
+    return np.concatenate([high, high, whole - high], axis=1).astype(np.float32)
+
+
 REFINE = refine_matrix()
 REFINE_SPLIT = np.concatenate([REFINE[:, 0::2], REFINE[:, 1::2]], axis=1)
 RESTRICT = restrict_matrix()
+OWN = np.stack([level_row_matrix(range(4 * z, 4 * z + 4), 8) for z in range(2)])
+ALL = level_row_matrix(range(8), 16)
 
 
 def dot(a, b):
@@ -103,43 +122,41 @@
     return jnp.concatenate(parts, axis=1)
 
 
-def fine_columns(high, low, matrix_ref):
+def by_levels_rows(matrix, fields):
+    high, low = split(fields.reshape(64, NX))
+    return dot(matrix, jnp.concatenate([high, low, high], axis=0))
+
+
+def windows(x, matrix_ref, halves):
+    high, low = split(x)
     parts = []
     for b in range(-1, 4):
-        window = slice(max(128 * b, 0), min(128 * b + 256, NX))
+        w = slice(max(128 * b, 0), min(128 * b + 256, NX))
         if b == -1:
-            matrix = matrix_ref[128:256, :]
+            matrix = matrix_ref[128:256, :] if halves else matrix_ref[128:256, 128:256]
         elif b == 3:
-            matrix = matrix_ref[0:128, :]
+            matrix = matrix_ref[0:128, :] if halves else matrix_ref[0:128, 0:128]
         else:
             matrix = matrix_ref[...]
-        parts.append((b, window, matrix))
-    return [dot(high[:, w], m) + dot(low[:, w], m) for _, w, m in parts]
+        parts.append(dot(jnp.concatenate([high[:, w], low[:, w]], axis=1), jnp.concatenate([matrix, matrix], axis=0)))
+    return parts
 
 
 def refined_rows(x, matrix_ref):
-    high, low = split(x)
-    parts = []
-    parts.append((high[:, :128], low[:, :128], matrix_ref[128:256, 128:256]))
-    for b in range(3):
-        w = slice(128 * b, 128 * b + 256)
-        parts.append((high[:, w], low[:, w], matrix_ref[...]))
-    parts.append((high[:, 384:], low[:, 384:], matrix_ref[0:128, 0:128]))
-    return jnp.concatenate([dot(h, m) + dot(l, m) for h, l, m in parts], axis=1)
-
-
-def heat_mean(planes, keep, matrix_ref):
-    high, low = split(jnp.concatenate(planes, axis=0))
+    return jnp.concatenate(windows(x, matrix_ref, False), axis=1)
+
+
+def heat_mean(x, keep, matrix_ref):
     sums = []
-    for t in fine_columns(high, low, matrix_ref):
-        q = t * (1.0 + 0.5 * t)
-        q = q[:, :128] + q[:, 128:]
-        sums.append(sum(q[keep * j : keep * j + keep] for j in range(len(planes))))
-    rolled = [pltpu.roll(s, 64, 1) for s in sums]
+    for t in windows(x, matrix_ref, True):
+        total = 0.0
+        for j in range(4):
+            for h in range(2):
+                piece = t[keep * j : keep * j + keep, 128 * h : 128 * h + 128]
+                total = total + piece * (1.0 + 0.5 * piece)
+        sums.append(pltpu.roll(total, 64, 1))
     low_half = iota((keep, 128), 1) < 64
-    return 0.125 * jnp.concatenate(
-        [jnp.where(low_half, rolled[c], rolled[c + 1]) for c in range(4)], axis=1
-    )
+    return 0.125 * jnp.concatenate([jnp.where(low_half, sums[c], sums[c + 1]) for c in range(4)], axis=1)
 
 
 def upwind(speed, positive, below, above):
@@ -150,18 +167,12 @@
     return jnp.concatenate([ref[tile, rows, :], ref[tile + 1, rows, :]], axis=-1)
 
 
-def pack_kernel(flow_hbm, heat_hbm, salt_hbm, restrict_hbm, a_ref, g_ref, mean_ref, plane_ref,
-                tile, strip, restrict_ref, sems):
-    z = lax.axis_index("gz")
-    flow_in = [pltpu.make_async_copy(flow_hbm, tile.at[pl.ds(0, 3)], sems.at[0])]
-    flow_in.append(pltpu.make_async_copy(heat_hbm, tile.at[3], sems.at[1]))
-    salt_in = [
-        pltpu.make_async_copy(salt_hbm.at[:, :, pl.ds(128 * c, 128)], strip.at[c], sems.at[3 + c]) for c in range(8)
-    ]
-    salt_in.append(pltpu.make_async_copy(restrict_hbm, restrict_ref, sems.at[2]))
-    for copy in flow_in + salt_in:
+def turn_kernel(flow_hbm, heat_hbm, a_ref, tile, sems):
+    copies = [pltpu.make_async_copy(flow_hbm, tile.at[pl.ds(0, 3)], sems.at[0])]
+    copies.append(pltpu.make_async_copy(heat_hbm, tile.at[3], sems.at[1]))
+    for copy in copies:
         copy.start()
-    for copy in flow_in:
+    for copy in copies:
         copy.wait()
     for lv in range(2):
         turned = jnp.concatenate([tile[f, lv] for f in range(4)], axis=0).T
@@ -169,8 +180,13 @@
             piece = turned[8 * j : 8 * j + 8]
             a_ref[j, 0, lv] = piece
             a_ref[j, 1, lv] = piece
-    for copy in salt_in:
-        copy.wait()
+
+
+def pack_kernel(salt_ref, restrict_ref, g_ref, mean_ref, plane_ref, strip):
+    z = lax.axis_index("gz")
+    for l in range(4):
+        for c in range(8):
+            strip[c, l] = salt_ref[l, :, 128 * c : 128 * c + 128]
     for l in range(4):
         for q in range(2):
             for c in range(8):
@@ -269,7 +285,7 @@
 
 
 def coarse_kernel(
-    c_ref, near_ref, far_ref, plane_ref, g_ref, refine_ref, refine_split_ref, restrict_ref,
+    c_ref, near_ref, far_ref, plane_ref, g_ref, refine_ref, refine_split_ref, restrict_ref, own_ref, all_ref,
     msg_ref, cp, mp, salt_mid, ur_ref, dr_ref, vel,
 ):
     z = lax.axis_index("gz")
@@ -288,20 +304,15 @@
         for m in range(4):
             cp[f, m + 2, 0:8, :] = c_ref[f, m]
             cp[f, m + 2, 8:16, :] = rim_of(ur_ref, dr_ref, f, m)
+    own_matrix = own_ref[z]
     for f in range(3):
-        for m in range(2):
-            for p in range(2):
-                even, odd = refine_rows(levels_of(cp, f, 2 * z + m, p), 8)
-                vel[f, 2 * m + p] = refined_rows(jnp.concatenate([even, odd], axis=0), refine_ref)
+        vel[f] = refined_rows(by_levels_rows(own_matrix, cp[f, 2:6]), refine_ref)
     rows16 = iota((16, NX), 0)
     inside = ((rows16 < 8) | (rows16 >= 12) | (place != 127)) & ((rows16 < 12) | (place != 0))
+    heat = by_levels_rows(all_ref[...], cp[3, 2:6])
     for m in range(4):
-        planes = []
-        for p in range(2):
-            terms = [cp[3, m + p + k] if 2 <= m + p + k < 6 else None for k in range(4)]
-            planes.extend(refine_rows(weigh(EVEN if p == 0 else ODD, terms), 16))
         salt_mean = jnp.concatenate([c_ref[4, m], rim_of(ur_ref, dr_ref, 4, m)], axis=0)
-        buoyancy = heat_mean(planes, 16, refine_split_ref) - 0.8 * salt_mean
+        buoyancy = heat_mean(heat[64 * m : 64 * m + 64], 16, refine_split_ref) - 0.8 * salt_mean
         speeds = [cp[f, m + 2] for f in range(3)]
         positives = [s > 0 for s in speeds]
         for f in range(4):
@@ -324,18 +335,16 @@
                 near = wide(g_ref, 2 * q, slice(0, 8))
                 below = jnp.where(z == 1, near, 0.0) if l == 0 else plane_ref[l - 1, q]
                 above = jnp.where(z == 0, near, 0.0) if l == 3 else plane_ref[l + 1, q]
-                speeds = [vel[f, l, 8 * q : 8 * q + 8, :] for f in (0, 2, 1)]
+                speeds = [vel[f, 16 * l + 8 * q : 16 * l + 8 * q + 8, :] for f in (0, 2, 1)]
                 x = own[q]
                 mid = x + salt_step(x, below, above, around[q][0], around[q][1], speeds)
                 salt_mid[l, q] = mid
                 total = mid if total is None else total + mid
         totals.append(total)
     means = restrict(jnp.concatenate(totals, axis=0), restrict_ref[...])
+    heat = by_levels_rows(own_matrix, mp[3, 2:6])
     for m in range(2):
-        planes = []
-        for p in range(2):
-            planes.extend(refine_rows(levels_of(mp, 3, 2 * z + m, p), 8))
-        buoyancy = heat_mean(planes, 8, refine_split_ref) - 0.8 * means[8 * m : 8 * m + 8]
+        buoyancy = heat_mean(heat[32 * m : 32 * m + 32], 8, refine_split_ref) - 0.8 * means[8 * m : 8 * m + 8]
         at = 2 * z + m + 2
         speeds = [mp[f, at, 0:8, :] for f in range(3)]
         positives = [s > 0 for s in speeds]
@@ -353,7 +362,7 @@
 
 
 def salt_kernel(
-    cp, mv, salt_mid_ref, plane_ref, ur_ref, dr_ref, g_ref, refine_ref, out_ref, vel, near_vel, strip,
+    cp, mv, salt_mid_ref, plane_ref, ur_ref, dr_ref, g_ref, refine_ref, own_ref, out_ref, vel, near_vel, strip,
 ):
     z = lax.axis_index("gz")
     place = lax.axis_index("gx") * 16 + lax.axis_index("gy")
@@ -368,10 +377,7 @@
         rims.extend(refine_rows(weigh(weights, [cp[f, 2 + k] for k in range(4)]), 8))
         near_vel[f] = refined_rows(jnp.concatenate(rims, axis=0), refine_ref)
     for f in range(3):
-        for m in range(2):
-            for p in range(2):
-                even, odd = refine_rows(levels_of(mv, f, 2 * z + m, p), 8)
-                vel[f, 2 * m + p] = refined_rows(jnp.concatenate([even, odd], axis=0), refine_ref)
+        vel[f] = refined_rows(by_levels_rows(own_ref[z], mv[f, 2:6]), refine_ref)
     line = iota((8, NF), 0)
     rim = [jnp.where(line == 0, edge_row(dr_ref, 2 * l), edge_row(ur_ref, 2 * l + 1)) for l in range(4)]
     near_rim = jnp.where(line == 0, near_edge(dr_ref), near_edge(ur_ref))
@@ -404,7 +410,7 @@
         after = pltpu.roll(jnp.where(line == 0, rim_mid[l], pair[0]), 7, 0)
         around = ((before, pair[1]), (pair[0], after))
         for q in range(2):
-            speeds = [vel[f, l, 8 * q : 8 * q + 8, :] for f in (0, 2, 1)]
+            speeds = [vel[f, 16 * l + 8 * q : 16 * l + 8 * q + 8, :] for f in (0, 2, 1)]
             below = jnp.where(z == 1, near_mid[q], 0.0) if l == 0 else salt_mid_ref[l - 1, q]
             above = jnp.where(z == 0, near_mid[q], 0.0) if l == 3 else salt_mid_ref[l + 1, q]
             x = pair[q]
@@ -427,7 +433,7 @@
 SPACES = {"h": pl.BlockSpec(memory_space=pltpu.HBM), "v": pl.BlockSpec(memory_space=pltpu.VMEM)}
 
 
-def call(kernel, name, ins, outs, scratch=()):
+def call(kernel, name, ins, outs, scratch=(), grant=16):
     return pl.pallas_call(
         kernel,
         name=name,
@@ -435,7 +441,7 @@
         out_specs=[SPACES["v"] for _ in outs],
         out_shape=[jax.ShapeDtypeStruct(s, F32) for s in outs],
         scratch_shapes=list(scratch),
-        compiler_params=pltpu.CompilerParams(vmem_limit_bytes=16 * 2**20),
+        compiler_params=pltpu.CompilerParams(vmem_limit_bytes=grant * 2**20),
     )
 
 
@@ -451,18 +457,19 @@
     refine = jnp.asarray(REFINE, BF16)
     refine_split = jnp.asarray(REFINE_SPLIT, BF16)
     restrict_m = jnp.asarray(RESTRICT, BF16)
-    a, g, means, planes = call(
-        pack_kernel,
-        "pack",
-        "hhhh",
-        [(16, 2, 2, 8, 128), (10, 8, NX), (2, 8, NX), (4, 2, 8, NF)],
-        [
-            vmem((4, 2, 32, 128), F32),
-            vmem((8, 4, 16, 128), F32),
-            vmem((256, 128), BF16),
-            pltpu.SemaphoreType.DMA((11,)),
-        ],
-    )(flow, heat, salt, restrict_m)
+    own_levels = jnp.asarray(OWN, BF16)
+    all_levels = jnp.asarray(ALL, BF16)
+    (a,) = call(
+        turn_kernel,
+        "turn",
+        "hh",
+        [(16, 2, 2, 8, 128)],
+        [vmem((4, 2, 32, 128), F32), pltpu.SemaphoreType.DMA((2,))],
+        grant=60,
+    )(flow, heat)
+    g, means, planes = call(
+        pack_kernel, "pack", "vv", [(10, 8, NX), (2, 8, NX), (4, 2, 8, NF)], [vmem((8, 4, 16, 128), F32)]
+    )(salt, restrict_m)
     g = swap(g, "gz", 2, 0)
     d = lax.all_to_all(a.reshape(32, 2, 8, 128), ("gy", "gz"), 0, 0, tiled=True)
     rims = [(13, 8, NX)] * 2
@@ -475,18 +482,18 @@
     msg, cp, mp, salt_mid, u, v = call(
         coarse_kernel,
         "coarse",
-        "vvvvvvvv",
+        "vvvvvvvvvv",
         [(16, 2, 8, 128)] + fields + [(4, 2, 8, NF)] + rims,
-        [vmem((3, 4, 16, NF), F32)],
-    )(c, near, far, planes, g, refine, refine_split, restrict_m)
+        [vmem((3, 64, NF), F32)],
+    )(c, near, far, planes, g, refine, refine_split, restrict_m, own_levels, all_levels)
     back = lax.all_to_all(msg, "gy", 0, 0, tiled=True)
     (salt_end,) = call(
         salt_kernel,
         "salt",
-        "vvvvvvvv",
+        "vvvvvvvvv",
         [(4, 16, NF)],
-        [vmem((3, 4, 16, NF), F32), vmem((3, 48, NF), F32), vmem((8, 4, 16, 128), F32)],
-    )(cp, mp, salt_mid, planes, u, v, g, refine)
+        [vmem((3, 64, NF), F32), vmem((3, 48, NF), F32), vmem((8, 4, 16, 128), F32)],
+    )(cp, mp, salt_mid, planes, u, v, g, refine, own_levels)
     flow_end, heat_end = call(unpack_kernel, "unpack", "v", [(3, 2, 32, 128), (2, 32, 128)])(back)
     return flow_end, heat_end, salt_end
 

time: 59.9 us -> 56.3 us (0.940)
  local copies, waits for them, and re-layouts: 4.12 us -> 0.68 us
  Pallas kernels: 9.59 us -> 8.82 us
  waiting for transfers between devices: 21.8 us -> 22.4 us
    unnamed x16 -> x14, local copies, waits for them, and re-layouts: 4.12 us -> 0.68 us
    pallas_call x3 -> x4, Pallas kernels: 7.81 us -> 7.03 us  [the longest x1 2.85 us: on_device(): call(coarse_kernel, 'coarse', 'vvvvvvvvvv', [(16, 2, 8, 128)] + fields +...]
    all_to_all x1, waiting for transfers between devices: 6.13 us -> 6.91 us  [on_device(): back = lax.all_to_all(msg, 'gy', 0, 0, tiled=True)]
  transfers between devices with their start and end apart: 5 -> 5, of which waited for: 4 -> 4; matrix products, arithmetic and copies ran while one was open for 0% -> 0% of each run, Pallas kernels for 5% -> 4%
where the time goes in v2:
time: 56.3 us; the launch traced here: 56 us
  starting transfers between devices  23.4 us (42%)
  waiting for transfers between devices  22.4 us (40%)
  Pallas kernels  8.82 us (16%)
  between operations  0.72 us (1%)
  local copies, waits for them, and re-layouts  0.68 us (1%)
    ppermute x3, waiting for transfers between devices, swap(): return lax.ppermute(x, axes, pairs)  11.9 us
    all_to_all x1, starting transfers between devices, on_device(): d = lax.all_to_all(a.reshape(32, 2, 8, 128), ('gy', 'gz'), 0, 0, tiled=True)  10.5 us
    all_to_all x1, starting transfers between devices, on_device(): back = lax.all_to_all(msg, 'gy', 0, 0, tiled=True)  9.02 us
    all_to_all x1, waiting for transfers between devices, on_device(): back = lax.all_to_all(msg, 'gy', 0, 0, tiled=True)  6.91 us
    ppermute x3, starting transfers between devices, swap(): return lax.ppermute(x, axes, pairs)  3.88 us
    all_to_all x1, waiting for transfers between devices, on_device(): d = lax.all_to_all(a.reshape(32, 2, 8, 128), ('gy', 'gz'), 0, 0, tiled=True)  3.62 us
    pallas_call x1, Pallas kernels, on_device(): call(coarse_kernel, 'coarse', 'vvvvvvvvvv', [(16, 2, 8, 128)] + fields +...  2.85 us
    pallas_call x1, Pallas kernels, on_device(): call(salt_kernel, 'salt', 'vvvvvvvvv', [(4, 16, NF)], [vmem((3, 64, NF),...  2.27 us
  transfers between devices with their start and end apart: 5, of which 4 were waited for; matrix products, arithmetic and copies ran while one was open for 0% of the time, Pallas kernels for 4%

profile of v2, /device:TPU:7, one launch (start us, length us, event | category | flops | bytes accessed | tf_op | source)
XLA Modules:
  0.0 56.0 jit_solution(5665970520989743522)
XLA Ops:
  0.6 1.7 %turn.1 = f32[16,2,2,8,128]{4,3,2,1,0:T(8,128)} custom-call(f32[3,2,32,128]{3,2,1,0:T(8,128)} %flow_hbm.1, f32[2,32,128]{2,1,0:T(8,128)} %heat_hbm.1), custom_call_target="tpu_custom_call" | custom-call | tf_op jit(solution)/shard_map/turn/pallas_call | solution.py:462
  2.4 0.0 copy-start.2
  2.4 0.0 copy-start.3
  2.4 10.5 %all-to-all-start = ((f32[32,2,8,128]{3,2,1,0:T(8,128)}), f32[32,2,8,128]{3,2,1,0:T(8,128)S(1)}, u32[]{:S(2)}, u32[]{:S(2)}) async-start(f32[32,2,8,128]{3,2,1,0:T(8,128)} %bitcast.3), calls=%async_computation | async-start | bytes 524288 | tf_op jit(solution)/shard_map/all_to_all | solution.py:474
  12.9 0.0 copy-done.2
  12.9 0.0 copy-done.3
  12.9 0.2 pack.1
  13.1 0.2 collective-permute-start
  13.3 6.8 %collective-permute-done.g_ref = f32[10,8,512]{2,1,0:T(8,128)S(1)} collective-permute-done((f32[10,8,512]{2,1,0:T(8,128)S(1)}, f32[10,8,512]{2,1,0:T(8,128)S(1)}, u32[]{:S(2)}, u32[]{:S(2)}) %collective-permute-start) | collective-permute-done | bytes 163872 | tf_op jit(solution)/shard_map/ppermute | solution.py:452
  20.1 3.6 %all-to-all-done = f32[32,2,8,128]{3,2,1,0:T(8,128)S(1)} async-done(((f32[32,2,8,128]{3,2,1,0:T(8,128)}), f32[32,2,8,128]{3,2,1,0:T(8,128)S(1)}, u32[]{:S(2)}, u32[]{:S(2)}) %all-to-all-start) | async-done | bytes 262176 | tf_op jit(solution)/shard_map/all_to_all | solution.py:474
  23.8 0.0 copy-start
  23.8 0.0 copy-start.1
  23.8 0.0 copy-start.5
  23.8 0.0 copy-start.6
  23.8 1.0 %send.1 = (f32[5,4,8,512]{3,2,1,0:T(8,128)S(1)}, f32[13,8,512]{2,1,0:T(8,128)S(1)}, f32[13,8,512]{2,1,0:T(8,128)S(1)}, f32[13,8,512]{2,1,0:T(8,128)}, f32[13,8,512]{2,1,0:T(8,128)}) custom-call(f32[16,4,8,128]{3,2,1,0:T(8,128)S(1)} %bitcast.2, f32[4,2,8,1024]{3,2,1,0:T(8,128)S(1)} %get-tuple-element.17.plane_ref, ...), custom_call_target="tpu_custom_call" | custom-call | tf_op jit(solution)/shard_map/send/pallas_call | solution.py:476
  24.8 1.6 %collective-permute-start.1 = (f32[13,8,512]{2,1,0:T(8,128)S(1)}, f32[13,8,512]{2,1,0:T(8,128)S(1)}, u32[]{:S(2)}, u32[]{:S(2)}) collective-permute-start(f32[13,8,512]{2,1,0:T(8,128)S(1)} %get-tuple-element.21), channel_id=1, source_target_pairs={{0,2},{2,0},{4,6},{6,4},{8,10},{10,8},{12,14},{14,12},{16,18},{18,... | collective-permute-start | bytes 638984 | tf_op jit(solution)/shard_map/ppermute | solution.py:452
  26.4 2.1 %collective-permute-start.2 = (f32[13,8,512]{2,1,0:T(8,128)S(1)}, f32[13,8,512]{2,1,0:T(8,128)S(1)}, u32[]{:S(2)}, u32[]{:S(2)}) collective-permute-start(f32[13,8,512]{2,1,0:T(8,128)S(1)} %get-tuple-element.22), channel_id=1, source_target_pairs={{2,4},{4,2},{6,8},{8,6},{10,12},{12,10},{14,16},{16,14},{18,20},{2... | collective-permute-start | bytes 638984 | tf_op jit(solution)/shard_map/ppermute | solution.py:452
  28.5 0.0 collective-permute-done.1.near_ref
  28.5 5.0 %collective-permute-done.2.far_ref = f32[13,8,512]{2,1,0:T(8,128)S(1)} collective-permute-done((f32[13,8,512]{2,1,0:T(8,128)S(1)}, f32[13,8,512]{2,1,0:T(8,128)S(1)}, u32[]{:S(2)}, u32[]{:S(2)}) %collective-permute-start.2) | collective-permute-done | bytes 213024 | tf_op jit(solution)/shard_map/ppermute | solution.py:452
  33.6 0.0 copy-done
  33.6 0.0 copy-done.1
  33.6 0.0 copy-done.5
  33.6 0.0 copy-done.6
  33.6 2.9 %coarse.1 = (f32[16,2,8,128]{3,2,1,0:T(8,128)S(1)}, f32[4,8,16,512]{3,2,1,0:T(8,128)S(1)}, f32[4,8,16,512]{3,2,1,0:T(8,128)S(1)}, f32[4,2,8,1024]{3,2,1,0:T(8,12...) custom-call(f32[5,4,8,512]{3,2,1,0:T(8,128)S(1)} %get-tuple-element.20.c_ref, ...), custom_call_target="tpu_custom_call" | custom-call | tf_op jit(solution)/shard_map/coarse/pallas_call | solution.py:482
  36.4 0.0 copy-start.4
  36.4 0.7 %copy-done.4 = f32[16,2,8,128]{3,2,1,0:T(8,128)} copy-done((f32[16,2,8,128]{3,2,1,0:T(8,128)}, f32[16,2,8,128]{3,2,1,0:T(8,128)S(1)}, u32[]{:S(2)}) %copy-start.4) | copy-done | bytes 131096
  37.1 9.0 %all-to-all-start.1 = ((f32[16,2,8,128]{3,2,1,0:T(8,128)}), f32[16,2,8,128]{3,2,1,0:T(8,128)S(1)}, u32[]{:S(2)}, u32[]{:S(2)}) async-start(f32[16,2,8,128]{3,2,1,0:T(8,128)} %copy-done.4), calls=%async_computation.1 | async-start | bytes 262144 | tf_op jit(solution)/shard_map/all_to_all | solution.py:489
  46.1 2.3 %salt.1 = f32[4,16,1024]{2,1,0:T(8,128)} custom-call(f32[4,8,16,512]{3,2,1,0:T(8,128)S(1)} %get-tuple-element.26.cp, f32[4,8,16,512]{3,2,1,0:T(8,128)S(1)} %get-tuple-element.27.mv, f32[4,2,8,1024]{3,2,1,0:T(8,128)S(1)} %get-tuple-element.28.salt_mid_ref, f32[4,2,8,1024]{3,2,1,0:T(8,128)S(1)} %get-tuple-element.17.plane_ref, ...), custom_call_target="tpu_custom_call" | custom-call | tf_op jit(solution)/shard_map/salt/pallas_call | solution.py:490
  48.4 6.9 %all-to-all-done.1.x_ref = f32[16,2,8,128]{3,2,1,0:T(8,128)S(1)} async-done(((f32[16,2,8,128]{3,2,1,0:T(8,128)}), f32[16,2,8,128]{3,2,1,0:T(8,128)S(1)}, u32[]{:S(2)}, u32[]{:S(2)}) %all-to-all-start.1) | async-done | bytes 131104 | tf_op jit(solution)/shard_map/all_to_all | solution.py:489
  55.3 0.7 %unpack.1 = (f32[3,2,32,128]{3,2,1,0:T(8,128)}, f32[2,32,128]{2,1,0:T(8,128)}) custom-call(f32[16,2,8,128]{3,2,1,0:T(8,128)S(1)} %all-to-all-done.1.x_ref), custom_call_target="tpu_custom_call" | custom-call | tf_op jit(solution)/shard_map/unpack/pallas_call | solution.py:497
Async XLA Ops:
  2.4 10.5 %copy-start.2 = (f32[4,16,1024]{2,1,0:T(8,128)S(1)}, f32[4,16,1024]{2,1,0:T(8,128)}, u32[]{:S(2)}) copy-start(f32[4,16,1024]{2,1,0:T(8,128)} %salt_ref.1) | copy-start | bytes 786436
  2.4 10.5 %copy-start.3 = (bf16[256,128]{1,0:T(8,128)(2,1)S(1)}, bf16[256,128]{1,0:T(8,128)(2,1)}, u32[]{:S(2)}) copy-start(bf16[256,128]{1,0:T(8,128)(2,1)} %constant.12.clone.restrict_ref) | copy-start | bytes 196612
  2.4 21.4 %all-to-all-start = ((f32[32,2,8,128]{3,2,1,0:T(8,128)}), f32[32,2,8,128]{3,2,1,0:T(8,128)S(1)}, u32[]{:S(2)}, u32[]{:S(2)}) async-start(f32[32,2,8,128]{3,2,1,0:T(8,128)} %bitcast.3), calls=%async_computation | async-start | bytes 524288 | tf_op jit(solution)/shard_map/all_to_all | solution.py:474
  13.1 7.0 %collective-permute-start = (f32[10,8,512]{2,1,0:T(8,128)S(1)}, f32[10,8,512]{2,1,0:T(8,128)S(1)}, u32[]{:S(2)}, u32[]{:S(2)}) collective-permute-start(f32[10,8,512]{2,1,0:T(8,128)S(1)} %get-tuple-element.19), channel_id=1, source_target_pairs={{0,1},{1,0},{2,3},{3,2},{4,5},{5,4},{6,7},{7,6},{8,9},{9,8},{10,11... | collective-permute-start | bytes 491528 | tf_op jit(solution)/shard_map/ppermute | solution.py:452
  23.8 9.8 %copy-start = (bf16[256,256]{1,0:T(8,128)(2,1)S(1)}, bf16[256,256]{1,0:T(8,128)(2,1)}, u32[]{:S(2)}) copy-start(bf16[256,256]{1,0:T(8,128)(2,1)} %constant.10.clone.refine_ref) | copy-start | bytes 393220
  23.8 9.8 %copy-start.1 = (bf16[2,64,192]{2,1,0:T(8,128)(2,1)S(1)}, bf16[2,64,192]{2,1,0:T(8,128)(2,1)}, u32[]{:S(2)}) copy-start(bf16[2,64,192]{2,1,0:T(8,128)(2,1)} %constant.13.clone.own_ref) | copy-start | bytes 147460
  23.8 9.8 %copy-start.5 = (bf16[256,192]{1,0:T(8,128)(2,1)S(1)}, bf16[256,192]{1,0:T(8,128)(2,1)}, u32[]{:S(2)}) copy-start(bf16[256,192]{1,0:T(8,128)(2,1)} %constant.14.clone.all_ref) | copy-start | bytes 294916
  23.8 9.8 %copy-start.6 = (bf16[256,256]{1,0:T(8,128)(2,1)S(1)}, bf16[256,256]{1,0:T(8,128)(2,1)}, u32[]{:S(2)}) copy-start(bf16[256,256]{1,0:T(8,128)(2,1)} %constant.11.clone.refine_split_ref) | copy-start | bytes 393220
  24.8 3.7 %collective-permute-start.1 = (f32[13,8,512]{2,1,0:T(8,128)S(1)}, f32[13,8,512]{2,1,0:T(8,128)S(1)}, u32[]{:S(2)}, u32[]{:S(2)}) collective-permute-start(f32[13,8,512]{2,1,0:T(8,128)S(1)} %get-tuple-element.21), channel_id=1, source_target_pairs={{0,2},{2,0},{4,6},{6,4},{8,10},{10,8},{12,14},{14,12},{16,18},{18,... | collective-permute-start | bytes 638984 | tf_op jit(solution)/shard_map/ppermute | solution.py:452
  26.4 7.2 %collective-permute-start.2 = (f32[13,8,512]{2,1,0:T(8,128)S(1)}, f32[13,8,512]{2,1,0:T(8,128)S(1)}, u32[]{:S(2)}, u32[]{:S(2)}) collective-permute-start(f32[13,8,512]{2,1,0:T(8,128)S(1)} %get-tuple-element.22), channel_id=1, source_target_pairs={{2,4},{4,2},{6,8},{8,6},{10,12},{12,10},{14,16},{16,14},{18,20},{2... | collective-permute-start | bytes 638984 | tf_op jit(solution)/shard_map/ppermute | solution.py:452
  36.4 0.7 %copy-start.4 = (f32[16,2,8,128]{3,2,1,0:T(8,128)}, f32[16,2,8,128]{3,2,1,0:T(8,128)S(1)}, u32[]{:S(2)}) copy-start(f32[16,2,8,128]{3,2,1,0:T(8,128)S(1)} %get-tuple-element.23) | copy-start | bytes 393220
  37.1 18.2 %all-to-all-start.1 = ((f32[16,2,8,128]{3,2,1,0:T(8,128)}), f32[16,2,8,128]{3,2,1,0:T(8,128)S(1)}, u32[]{:S(2)}, u32[]{:S(2)}) async-start(f32[16,2,8,128]{3,2,1,0:T(8,128)} %copy-done.4), calls=%async_computation.1 | async-start | bytes 262144 | tf_op jit(solution)/shard_map/all_to_all | solution.py:489

commit v3 on v2

--- a/solution.py
+++ b/solution.py
@@ -5,6 +5,7 @@
 from jax.experimental import pallas as pl
 from jax.experimental.pallas import tpu as pltpu
 from jax.sharding import PartitionSpec as P
+
 
 F32 = jnp.float32
 BF16 = jnp.bfloat16
@@ -80,7 +81,6 @@
 
 
 def left(x):
-    n = x.shape[1]
     return jnp.where(iota(x.shape, 1) == 0, 0.0, pltpu.roll(x, 1, 1))
 
 
@@ -182,7 +182,21 @@
             a_ref[j, 1, lv] = piece
 
 
-def pack_kernel(salt_ref, restrict_ref, g_ref, mean_ref, plane_ref, strip):
+def to_sides(near_ref, far_ref, tile, up, down):
+    leads = lax.rem(lax.axis_index("gy"), 2) == 0
+    near_ref[tile] = jnp.where(leads, up, down)
+    far_ref[tile] = jnp.where(leads, down, up)
+
+
+def few_rows(a, b, c, d):
+    line = iota((8, NX), 0)
+    out = jnp.where(line < 2, a, pltpu.roll(b, 2, 0))
+    if c is not None:
+        out = jnp.where(line < 4, out, jnp.where(line == 4, c, d))
+    return out
+
+
+def pack_kernel(salt_ref, restrict_ref, g_ref, mean_ref, plane_ref, near_ref, far_ref, strip, up, down):
     z = lax.axis_index("gz")
     for l in range(4):
         for c in range(8):
@@ -198,6 +212,17 @@
     for m in range(2):
         mean_ref[m] = means[8 * m : 8 * m + 8]
         g_ref[8 + m] = means[8 * m : 8 * m + 8]
+    for h in range(2):
+        w = slice(512 * h, 512 * h + 512)
+        for l in range(4):
+            for q in range(2):
+                k = 2 * l + q
+                down[h, k : k + 1, :] = plane_ref[l, q, 0:1, w]
+                up[h, k : k + 1, :] = plane_ref[l, q, 7:8, w]
+        to_sides(near_ref, far_ref, h, up[h], down[h])
+    low, high = (means[0:8], means[8:16])
+    rolled = few_rows(pltpu.roll(low, 2, 0), pltpu.roll(high, 2, 0), None, None)
+    to_sides(near_ref, far_ref, 2, rolled, few_rows(low, high, None, None))
     for near in range(2):
         level = jnp.where(z == 0, 3 - near, near)
         for q in range(2):
@@ -210,9 +235,8 @@
     return jnp.where(z == m // 2, mean_ref[m % 2], g_ref[8 + m % 2])
 
 
-def send_kernel(d_ref, plane_ref, mean_ref, g_ref, c_ref, near_ref, far_ref, up_ref, down_ref):
+def send_kernel(d_ref, mean_ref, g_ref, c_ref, near_ref, far_ref):
     z = lax.axis_index("gz")
-    leads = lax.rem(lax.axis_index("gy"), 2) == 0
     for m in range(4):
         for b in range(4):
             tiles = turn_blocks([d_ref[4 * b + j, m] for j in range(4)])
@@ -220,28 +244,19 @@
                 c_ref[f, m, :, 128 * b : 128 * b + 128] = tiles[f]
         c_ref[4, m] = mean_of(mean_ref, g_ref, z, m)
     first = iota((8, NX), 0) < 4
-    for f in range(5):
+    for f in range(4):
         for p in range(2):
             a = c_ref[f, 2 * p]
             b = c_ref[f, 2 * p + 1]
-            down_ref[2 * f + p] = jnp.where(first, a, pltpu.roll(b, 4, 0))
-            up_ref[2 * f + p] = jnp.where(first, pltpu.roll(a, 4, 0), b)
-    down_ref[12] = jnp.zeros((8, NX), F32)
-    up_ref[12] = jnp.zeros((8, NX), F32)
-    for h in range(2):
-        w = slice(512 * h, 512 * h + 512)
-        for l in range(4):
-            for q in range(2):
-                k = 2 * l + q
-                down_ref[10 + h, k : k + 1, :] = plane_ref[l, q, 0:1, w]
-                up_ref[10 + h, k : k + 1, :] = plane_ref[l, q, 7:8, w]
-        down_ref[12, h : h + 1, :] = g_ref[h, 0:1, :]
-        up_ref[12, h : h + 1, :] = g_ref[2 + h, 7:8, :]
-    for t in range(13):
-        up = up_ref[t]
-        down = down_ref[t]
-        near_ref[t] = jnp.where(leads, up, down)
-        far_ref[t] = jnp.where(leads, down, up)
+            down = jnp.where(first, a, pltpu.roll(b, 4, 0))
+            up = jnp.where(first, pltpu.roll(a, 4, 0), b)
+            to_sides(near_ref, far_ref, 2 * f + p, up, down)
+    low, high = (g_ref[8], g_ref[9])
+    rows = [jnp.broadcast_to(g_ref[h, 0:1, :], (8, NX)) for h in range(2)]
+    down = few_rows(low, high, rows[0], rows[1])
+    rows = [jnp.broadcast_to(g_ref[2 + h, 7:8, :], (8, NX)) for h in range(2)]
+    up = few_rows(pltpu.roll(low, 2, 0), pltpu.roll(high, 2, 0), rows[0], rows[1])
+    to_sides(near_ref, far_ref, 8, up, down)
 
 
 def coarse_rate(q, below, above, speeds, positives, diffusion, keep):
@@ -262,12 +277,12 @@
 
 
 def edge_row(ref, k):
-    whole = jnp.concatenate([ref[10, k : k + 1, :], ref[11, k : k + 1, :]], axis=-1)
+    whole = jnp.concatenate([ref[9, k : k + 1, :], ref[10, k : k + 1, :]], axis=-1)
     return jnp.broadcast_to(whole, (8, NF))
 
 
 def near_edge(ref):
-    whole = jnp.concatenate([ref[12, 0:1, :], ref[12, 1:2, :]], axis=-1)
+    whole = jnp.concatenate([ref[8, 4:5, :], ref[8, 5:6, :]], axis=-1)
     return jnp.broadcast_to(whole, (8, NF))
 
 
@@ -285,15 +300,15 @@
 
 
 def coarse_kernel(
-    c_ref, near_ref, far_ref, plane_ref, g_ref, refine_ref, refine_split_ref, restrict_ref, own_ref, all_ref,
+    c_ref, near_ref, far_ref, near_salt_ref, far_salt_ref, plane_ref, g_ref, refine_ref, refine_split_ref, restrict_ref, own_ref, all_ref,
     msg_ref, cp, mp, salt_mid, ur_ref, dr_ref, vel,
 ):
     z = lax.axis_index("gz")
     leads = lax.rem(lax.axis_index("gy"), 2) == 0
     place = lax.axis_index("gx") * 16 + lax.axis_index("gy")
-    for t in range(13):
-        near = near_ref[t]
-        far = far_ref[t]
+    for t in range(12):
+        near = near_ref[t] if t < 9 else near_salt_ref[t - 9]
+        far = far_ref[t] if t < 9 else far_salt_ref[t - 9]
         ur_ref[t] = jnp.where(leads, far, near)
         dr_ref[t] = jnp.where(leads, near, far)
     zero = jnp.zeros((16, NX), F32)
@@ -311,7 +326,16 @@
     inside = ((rows16 < 8) | (rows16 >= 12) | (place != 127)) & ((rows16 < 12) | (place != 0))
     heat = by_levels_rows(all_ref[...], cp[3, 2:6])
     for m in range(4):
-        salt_mean = jnp.concatenate([c_ref[4, m], rim_of(ur_ref, dr_ref, 4, m)], axis=0)
+        own_level = z == m // 2
+        below = jnp.where(own_level, dr_ref[11], dr_ref[8])
+        above = jnp.where(own_level, ur_ref[11], ur_ref[8])
+        if m % 2 == 1:
+            below = pltpu.roll(below, 6, 0)
+            above = pltpu.roll(above, 4, 0)
+        else:
+            above = pltpu.roll(above, 6, 0)
+        rim = jnp.where(iota((8, NX), 0) < 2, below, above)
+        salt_mean = jnp.concatenate([c_ref[4, m], rim], axis=0)
         buoyancy = heat_mean(heat[64 * m : 64 * m + 64], 16, refine_split_ref) - 0.8 * salt_mean
         speeds = [cp[f, m + 2] for f in range(3)]
         positives = [s > 0 for s in speeds]
@@ -433,10 +457,9 @@
 SPACES = {"h": pl.BlockSpec(memory_space=pltpu.HBM), "v": pl.BlockSpec(memory_space=pltpu.VMEM)}
 
 
-def call(kernel, name, ins, outs, scratch=(), grant=16):
+def call(kernel, ins, outs, scratch=(), grant=16):
     return pl.pallas_call(
         kernel,
-        name=name,
         in_specs=[SPACES[letter] for letter in ins],
         out_specs=[SPACES["v"] for _ in outs],
         out_shape=[jax.ShapeDtypeStruct(s, F32) for s in outs],
@@ -452,7 +475,7 @@
     return lax.ppermute(x, axes, pairs)
 
 
-def on_device(flow, heat, salt):
+def step(flow, heat, salt):
     vmem = pltpu.VMEM
     refine = jnp.asarray(REFINE, BF16)
     refine_split = jnp.asarray(REFINE_SPLIT, BF16)
@@ -460,44 +483,37 @@
     own_levels = jnp.asarray(OWN, BF16)
     all_levels = jnp.asarray(ALL, BF16)
     (a,) = call(
-        turn_kernel,
-        "turn",
-        "hh",
-        [(16, 2, 2, 8, 128)],
-        [vmem((4, 2, 32, 128), F32), pltpu.SemaphoreType.DMA((2,))],
-        grant=60,
+        turn_kernel, "hh", [(16, 2, 2, 8, 128)], [vmem((4, 2, 32, 128), F32), pltpu.SemaphoreType.DMA((2,))], grant=60
     )(flow, heat)
-    g, means, planes = call(
-        pack_kernel, "pack", "vv", [(10, 8, NX), (2, 8, NX), (4, 2, 8, NF)], [vmem((8, 4, 16, 128), F32)]
+    g, means, planes, near_salt, far_salt = call(
+        pack_kernel,
+        "vv",
+        [(10, 8, NX), (2, 8, NX), (4, 2, 8, NF), (3, 8, NX), (3, 8, NX)],
+        [vmem((8, 4, 16, 128), F32), vmem((2, 8, NX), F32), vmem((2, 8, NX), F32)],
     )(salt, restrict_m)
     g = swap(g, "gz", 2, 0)
+    near_salt = swap(near_salt, ("gx", "gy"), 128, 0)
+    far_salt = swap(far_salt, ("gx", "gy"), 128, 1)
     d = lax.all_to_all(a.reshape(32, 2, 8, 128), ("gy", "gz"), 0, 0, tiled=True)
-    rims = [(13, 8, NX)] * 2
-    c, near, far, _, _ = call(send_kernel, "send", "vvvv", [(5, 4, 8, NX)] + rims + rims)(
-        d.reshape(16, 4, 8, 128), planes, means, g
-    )
+    c, near, far = call(send_kernel, "vvv", [(5, 4, 8, NX), (9, 8, NX), (9, 8, NX)])(d.reshape(16, 4, 8, 128), means, g)
     near = swap(near, ("gx", "gy"), 128, 0)
     far = swap(far, ("gx", "gy"), 128, 1)
+    rims = [(12, 8, NX)] * 2
     fields = [(4, 8, 16, NX)] * 2
     msg, cp, mp, salt_mid, u, v = call(
-        coarse_kernel,
-        "coarse",
-        "vvvvvvvvvv",
-        [(16, 2, 8, 128)] + fields + [(4, 2, 8, NF)] + rims,
-        [vmem((3, 64, NF), F32)],
-    )(c, near, far, planes, g, refine, refine_split, restrict_m, own_levels, all_levels)
+        coarse_kernel, "vvvvvvvvvvvv", [(16, 2, 8, 128)] + fields + [(4, 2, 8, NF)] + rims, [vmem((3, 64, NF), F32)]
+    )(c, near, far, near_salt, far_salt, planes, g, refine, refine_split, restrict_m, own_levels, all_levels)
     back = lax.all_to_all(msg, "gy", 0, 0, tiled=True)
     (salt_end,) = call(
         salt_kernel,
-        "salt",
         "vvvvvvvvv",
         [(4, 16, NF)],
         [vmem((3, 64, NF), F32), vmem((3, 48, NF), F32), vmem((8, 4, 16, 128), F32)],
     )(cp, mp, salt_mid, planes, u, v, g, refine, own_levels)
-    flow_end, heat_end = call(unpack_kernel, "unpack", "v", [(3, 2, 32, 128), (2, 32, 128)])(back)
+    flow_end, heat_end = call(unpack_kernel, "v", [(3, 2, 32, 128), (2, 32, 128)])(back)
     return flow_end, heat_end, salt_end
 
 
 def solution(mesh):
     specs = (P(None, "gz", "gy", "gx"), P("gz", "gy", "gx"), P("gz", ("gx", "gy"), None))
-    return jax.shard_map(on_device, mesh=mesh, in_specs=specs, out_specs=specs, check_vma=False)
+    return jax.shard_map(step, mesh=mesh, in_specs=specs, out_specs=specs, check_vma=False)

time: 56.3 us -> 59.3 us (1.053)
  starting transfers between devices: 23.4 us -> 28.3 us
  waiting for transfers between devices: 22.4 us -> 21.1 us
  Pallas kernels: 8.82 us -> 8.06 us
    ppermute x3 -> x5, starting transfers between devices: 3.88 us -> 9.05 us  [swap(): return lax.ppermute(x, axes, pairs)]
    ppermute x3 -> x5, waiting for transfers between devices: 11.9 us -> 10.6 us  [swap(): return lax.ppermute(x, axes, pairs)]
    pallas_call x6, Pallas kernels: 8.82 us -> 8.06 us  [the longest x1 2.86 us: step(): call(coarse_kernel, 'vvvvvvvvvvvv', [(16, 2, 8, 128)] + fields + [(4, 2,...]
  transfers between devices with their start and end apart: 5 -> 7, of which waited for: 4 -> 4; matrix products, arithmetic and copies ran while one was open for 0% -> 0% of each run, Pallas kernels for 4% -> 4%
where the time goes in v3:
time: 59.3 us; the launch traced here: 58.9 us
  starting transfers between devices  28.3 us (48%)
  waiting for transfers between devices  21.1 us (36%)
  Pallas kernels  8.06 us (14%)
  between operations  0.75 us (1%)
  local copies, waits for them, and re-layouts  0.69 us (1%)
    ppermute x5, waiting for transfers between devices, swap(): return lax.ppermute(x, axes, pairs)  10.6 us
    all_to_all x1, starting transfers between devices, step(): d = lax.all_to_all(a.reshape(32, 2, 8, 128), ('gy', 'gz'), 0, 0, tiled=True)  10.5 us
    ppermute x5, starting transfers between devices, swap(): return lax.ppermute(x, axes, pairs)  9.05 us
    all_to_all x1, starting transfers between devices, step(): back = lax.all_to_all(msg, 'gy', 0, 0, tiled=True)  8.75 us
    all_to_all x1, waiting for transfers between devices, step(): back = lax.all_to_all(msg, 'gy', 0, 0, tiled=True)  6.91 us
    all_to_all x1, waiting for transfers between devices, step(): d = lax.all_to_all(a.reshape(32, 2, 8, 128), ('gy', 'gz'), 0, 0, tiled=True)  3.6 us
    pallas_call x1, Pallas kernels, step(): call(coarse_kernel, 'vvvvvvvvvvvv', [(16, 2, 8, 128)] + fields + [(4, 2,...  2.86 us
    pallas_call x1, Pallas kernels, step(): call(salt_kernel, 'vvvvvvvvv', [(4, 16, NF)], [vmem((3, 64, NF), F32), vm...  2.27 us
  transfers between devices with their start and end apart: 7, of which 4 were waited for; matrix products, arithmetic and copies ran while one was open for 0% of the time, Pallas kernels for 4%

profile of v3, /device:TPU:7, one launch (start us, length us, event | category | flops | bytes accessed | tf_op | source)
XLA Modules:
  0.0 58.9 jit_solution(8112086210363626356)
XLA Ops:
  0.6 1.7 %shard_map.103 = f32[16,2,2,8,128]{4,3,2,1,0:T(8,128)} custom-call(f32[3,2,32,128]{3,2,1,0:T(8,128)} %flow_hbm.1, f32[2,32,128]{2,1,0:T(8,128)} %heat_hbm.1), custom_call_target="tpu_custom_call" | custom-call | tf_op jit(solution)/shard_map/pallas_call | solution.py:485
  2.4 0.0 copy-start.2
  2.4 0.0 copy-start.3
  2.4 10.5 %all-to-all-start = ((f32[32,2,8,128]{3,2,1,0:T(8,128)}), f32[32,2,8,128]{3,2,1,0:T(8,128)S(1)}, u32[]{:S(2)}, u32[]{:S(2)}) async-start(f32[32,2,8,128]{3,2,1,0:T(8,128)} %bitcast.3), calls=%async_computation | async-start | bytes 524288 | tf_op jit(solution)/shard_map/all_to_all | solution.py:497
  12.9 0.0 copy-done.2
  12.9 0.0 copy-done.3
  12.9 0.2 shard_map.104
  13.1 0.2 collective-permute-start
  13.3 6.8 %collective-permute-done.g_ref = f32[10,8,512]{2,1,0:T(8,128)S(1)} collective-permute-done((f32[10,8,512]{2,1,0:T(8,128)S(1)}, f32[10,8,512]{2,1,0:T(8,128)S(1)}, u32[]{:S(2)}, u32[]{:S(2)}) %collective-permute-start) | collective-permute-done | bytes 163872 | tf_op jit(solution)/shard_map/ppermute | solution.py:475
  20.2 3.6 %all-to-all-done = f32[32,2,8,128]{3,2,1,0:T(8,128)S(1)} async-done(((f32[32,2,8,128]{3,2,1,0:T(8,128)}), f32[32,2,8,128]{3,2,1,0:T(8,128)S(1)}, u32[]{:S(2)}, u32[]{:S(2)}) %all-to-all-start) | async-done | bytes 262176 | tf_op jit(solution)/shard_map/all_to_all | solution.py:497
  23.8 0.0 copy-start
  23.8 0.0 copy-start.1
  23.8 0.0 copy-start.4
  23.8 0.0 copy-start.5
  23.8 0.3 shard_map.105
  24.0 1.7 %collective-permute-start.1 = (f32[9,8,512]{2,1,0:T(8,128)S(1)}, f32[9,8,512]{2,1,0:T(8,128)S(1)}, u32[]{:S(2)}, u32[]{:S(2)}) collective-permute-start(f32[9,8,512]{2,1,0:T(8,128)S(1)} %get-tuple-element.22), channel_id=1, source_target_pairs={{0,2},{2,0},{4,6},{6,4},{8,10},{10,8},{12,14},{14,12},{16,18},{18,... | collective-permute-start | bytes 442376 | tf_op jit(solution)/shard_map/ppermute | solution.py:475
  25.7 2.1 %collective-permute-start.2 = (f32[9,8,512]{2,1,0:T(8,128)S(1)}, f32[9,8,512]{2,1,0:T(8,128)S(1)}, u32[]{:S(2)}, u32[]{:S(2)}) collective-permute-start(f32[9,8,512]{2,1,0:T(8,128)S(1)} %get-tuple-element.23), channel_id=1, source_target_pairs={{2,4},{4,2},{6,8},{8,6},{10,12},{12,10},{14,16},{16,14},{18,20},{2... | collective-permute-start | bytes 442376 | tf_op jit(solution)/shard_map/ppermute | solution.py:475
  27.8 3.2 %collective-permute-start.3 = (f32[3,8,512]{2,1,0:T(8,128)S(1)}, f32[3,8,512]{2,1,0:T(8,128)S(1)}, u32[]{:S(2)}, u32[]{:S(2)}) collective-permute-start(f32[3,8,512]{2,1,0:T(8,128)S(1)} %get-tuple-element.24), channel_id=1, source_target_pairs={{0,2},{2,0},{4,6},{6,4},{8,10},{10,8},{12,14},{14,12},{16,18},{18,... | collective-permute-start | bytes 147464 | tf_op jit(solution)/shard_map/ppermute | solution.py:475
  31.0 1.9 %collective-permute-start.4 = (f32[3,8,512]{2,1,0:T(8,128)S(1)}, f32[3,8,512]{2,1,0:T(8,128)S(1)}, u32[]{:S(2)}, u32[]{:S(2)}) collective-permute-start(f32[3,8,512]{2,1,0:T(8,128)S(1)} %get-tuple-element.25), channel_id=1, source_target_pairs={{2,4},{4,2},{6,8},{8,6},{10,12},{12,10},{14,16},{16,14},{18,20},{2... | collective-permute-start | bytes 147464 | tf_op jit(solution)/shard_map/ppermute | solution.py:475
  32.9 0.0 collective-permute-done.3.near_salt_ref
  32.9 3.8 %collective-permute-done.4.far_salt_ref = f32[3,8,512]{2,1,0:T(8,128)S(1)} collective-permute-done((f32[3,8,512]{2,1,0:T(8,128)S(1)}, f32[3,8,512]{2,1,0:T(8,128)S(1)}, u32[]{:S(2)}, u32[]{:S(2)}) %collective-permute-start.4) | collective-permute-done | bytes 49184 | tf_op jit(solution)/shard_map/ppermute | solution.py:475
  36.7 0.0 collective-permute-done.1.near_ref
  36.7 0.0 collective-permute-done.2.far_ref
  36.7 0.0 copy-done
  36.7 0.0 copy-done.1
  36.7 0.0 copy-done.4
  36.7 0.0 copy-done.5
  36.7 2.9 %shard_map.106 = (f32[16,2,8,128]{3,2,1,0:T(8,128)S(1)}, f32[4,8,16,512]{3,2,1,0:T(8,128)S(1)}, f32[4,8,16,512]{3,2,1,0:T(8,128)S(1)}, f32[4,2,8,1024]{3,2,1,0:T...) custom-call(f32[5,4,8,512]{3,2,1,0:T(8,128)S(1)} %get-tuple-element.21.c_ref, ...), custom_call_target="tpu_custom_call" | custom-call | tf_op jit(solution)/shard_map/pallas_call | solution.py:503
  39.6 0.0 copy-start.6
  39.6 0.7 %copy-done.6 = f32[16,2,8,128]{3,2,1,0:T(8,128)} copy-done((f32[16,2,8,128]{3,2,1,0:T(8,128)}, f32[16,2,8,128]{3,2,1,0:T(8,128)S(1)}, u32[]{:S(2)}) %copy-start.6) | copy-done | bytes 131096
  40.3 8.8 %all-to-all-start.1 = ((f32[16,2,8,128]{3,2,1,0:T(8,128)}), f32[16,2,8,128]{3,2,1,0:T(8,128)S(1)}, u32[]{:S(2)}, u32[]{:S(2)}) async-start(f32[16,2,8,128]{3,2,1,0:T(8,128)} %copy-done.6), calls=%async_computation.1 | async-start | bytes 262144 | tf_op jit(solution)/shard_map/all_to_all | solution.py:506
  49.0 2.3 %shard_map.108 = f32[4,16,1024]{2,1,0:T(8,128)} custom-call(f32[4,8,16,512]{3,2,1,0:T(8,128)S(1)} %get-tuple-element.30.cp, f32[4,8,16,512]{3,2,1,0:T(8,128)S(1)} %get-tuple-element.31.mv, f32[4,2,8,1024]{3,2,1,0:T(8,128)S(1)} %get-tuple-element.32.salt_mid_ref, f32[4,2,8,1024]{3,2,1,0:T(8,128)S(1)} %get-tuple-element.26.plane_ref, ...), custom_call_target="tpu_custom_call" | custom-call | tf_op jit(solution)/shard_map/pallas_call | solution.py:507
  51.3 6.9 %all-to-all-done.1.x_ref = f32[16,2,8,128]{3,2,1,0:T(8,128)S(1)} async-done(((f32[16,2,8,128]{3,2,1,0:T(8,128)}), f32[16,2,8,128]{3,2,1,0:T(8,128)S(1)}, u32[]{:S(2)}, u32[]{:S(2)}) %all-to-all-start.1) | async-done | bytes 131104 | tf_op jit(solution)/shard_map/all_to_all | solution.py:506
  58.2 0.7 %shard_map.107 = (f32[3,2,32,128]{3,2,1,0:T(8,128)}, f32[2,32,128]{2,1,0:T(8,128)}) custom-call(f32[16,2,8,128]{3,2,1,0:T(8,128)S(1)} %all-to-all-done.1.x_ref), custom_call_target="tpu_custom_call" | custom-call | tf_op jit(solution)/shard_map/pallas_call | solution.py:513
Async XLA Ops:
  2.4 10.5 %copy-start.2 = (bf16[256,128]{1,0:T(8,128)(2,1)S(1)}, bf16[256,128]{1,0:T(8,128)(2,1)}, u32[]{:S(2)}) copy-start(bf16[256,128]{1,0:T(8,128)(2,1)} %constant.12.clone.restrict_ref) | copy-start | bytes 196612
  2.4 10.5 %copy-start.3 = (f32[4,16,1024]{2,1,0:T(8,128)S(1)}, f32[4,16,1024]{2,1,0:T(8,128)}, u32[]{:S(2)}) copy-start(f32[4,16,1024]{2,1,0:T(8,128)} %salt_ref.1) | copy-start | bytes 786436
  2.4 21.4 %all-to-all-start = ((f32[32,2,8,128]{3,2,1,0:T(8,128)}), f32[32,2,8,128]{3,2,1,0:T(8,128)S(1)}, u32[]{:S(2)}, u32[]{:S(2)}) async-start(f32[32,2,8,128]{3,2,1,0:T(8,128)} %bitcast.3), calls=%async_computation | async-start | bytes 524288 | tf_op jit(solution)/shard_map/all_to_all | solution.py:497
  13.1 7.0 %collective-permute-start = (f32[10,8,512]{2,1,0:T(8,128)S(1)}, f32[10,8,512]{2,1,0:T(8,128)S(1)}, u32[]{:S(2)}, u32[]{:S(2)}) collective-permute-start(f32[10,8,512]{2,1,0:T(8,128)S(1)} %get-tuple-element.20), channel_id=1, source_target_pairs={{0,1},{1,0},{2,3},{3,2},{4,5},{5,4},{6,7},{7,6},{8,9},{9,8},{10,11... | collective-permute-start | bytes 491528 | tf_op jit(solution)/shard_map/ppermute | solution.py:475
  23.8 12.9 %copy-start = (bf16[256,256]{1,0:T(8,128)(2,1)S(1)}, bf16[256,256]{1,0:T(8,128)(2,1)}, u32[]{:S(2)}) copy-start(bf16[256,256]{1,0:T(8,128)(2,1)} %constant.10.clone.refine_ref) | copy-start | bytes 393220
  23.8 12.9 %copy-start.1 = (bf16[2,64,192]{2,1,0:T(8,128)(2,1)S(1)}, bf16[2,64,192]{2,1,0:T(8,128)(2,1)}, u32[]{:S(2)}) copy-start(bf16[2,64,192]{2,1,0:T(8,128)(2,1)} %constant.13.clone.own_ref) | copy-start | bytes 147460
  23.8 12.9 %copy-start.4 = (bf16[256,192]{1,0:T(8,128)(2,1)S(1)}, bf16[256,192]{1,0:T(8,128)(2,1)}, u32[]{:S(2)}) copy-start(bf16[256,192]{1,0:T(8,128)(2,1)} %constant.14.clone.all_ref) | copy-start | bytes 294916
  23.8 13.0 %copy-start.5 = (bf16[256,256]{1,0:T(8,128)(2,1)S(1)}, bf16[256,256]{1,0:T(8,128)(2,1)}, u32[]{:S(2)}) copy-start(bf16[256,256]{1,0:T(8,128)(2,1)} %constant.11.clone.refine_split_ref) | copy-start | bytes 393220
  24.0 12.6 %collective-permute-start.1 = (f32[9,8,512]{2,1,0:T(8,128)S(1)}, f32[9,8,512]{2,1,0:T(8,128)S(1)}, u32[]{:S(2)}, u32[]{:S(2)}) collective-permute-start(f32[9,8,512]{2,1,0:T(8,128)S(1)} %get-tuple-element.22), channel_id=1, source_target_pairs={{0,2},{2,0},{4,6},{6,4},{8,10},{10,8},{12,14},{14,12},{16,18},{18,... | collective-permute-start | bytes 442376 | tf_op jit(solution)/shard_map/ppermute | solution.py:475
  25.7 11.0 %collective-permute-start.2 = (f32[9,8,512]{2,1,0:T(8,128)S(1)}, f32[9,8,512]{2,1,0:T(8,128)S(1)}, u32[]{:S(2)}, u32[]{:S(2)}) collective-permute-start(f32[9,8,512]{2,1,0:T(8,128)S(1)} %get-tuple-element.23), channel_id=1, source_target_pairs={{2,4},{4,2},{6,8},{8,6},{10,12},{12,10},{14,16},{16,14},{18,20},{2... | collective-permute-start | bytes 442376 | tf_op jit(solution)/shard_map/ppermute | solution.py:475
  27.8 5.1 %collective-permute-start.3 = (f32[3,8,512]{2,1,0:T(8,128)S(1)}, f32[3,8,512]{2,1,0:T(8,128)S(1)}, u32[]{:S(2)}, u32[]{:S(2)}) collective-permute-start(f32[3,8,512]{2,1,0:T(8,128)S(1)} %get-tuple-element.24), channel_id=1, source_target_pairs={{0,2},{2,0},{4,6},{6,4},{8,10},{10,8},{12,14},{14,12},{16,18},{18,... | collective-permute-start | bytes 147464 | tf_op jit(solution)/shard_map/ppermute | solution.py:475
  31.0 5.7 %collective-permute-start.4 = (f32[3,8,512]{2,1,0:T(8,128)S(1)}, f32[3,8,512]{2,1,0:T(8,128)S(1)}, u32[]{:S(2)}, u32[]{:S(2)}) collective-permute-start(f32[3,8,512]{2,1,0:T(8,128)S(1)} %get-tuple-element.25), channel_id=1, source_target_pairs={{2,4},{4,2},{6,8},{8,6},{10,12},{12,10},{14,16},{16,14},{18,20},{2... | collective-permute-start | bytes 147464 | tf_op jit(solution)/shard_map/ppermute | solution.py:475
  39.6 0.7 %copy-start.6 = (f32[16,2,8,128]{3,2,1,0:T(8,128)}, f32[16,2,8,128]{3,2,1,0:T(8,128)S(1)}, u32[]{:S(2)}) copy-start(f32[16,2,8,128]{3,2,1,0:T(8,128)S(1)} %get-tuple-element.27) | copy-start | bytes 393220
  40.3 17.9 %all-to-all-start.1 = ((f32[16,2,8,128]{3,2,1,0:T(8,128)}), f32[16,2,8,128]{3,2,1,0:T(8,128)S(1)}, u32[]{:S(2)}, u32[]{:S(2)}) async-start(f32[16,2,8,128]{3,2,1,0:T(8,128)} %copy-done.6), calls=%async_computation.1 | async-start | bytes 262144 | tf_op jit(solution)/shard_map/all_to_all | solution.py:506

commit v4 on v3

--- a/solution.py
+++ b/solution.py
@@ -76,12 +76,17 @@
 
 
 def right(x):
-    n = x.shape[1]
-    return jnp.where(iota(x.shape, 1) == n - 1, 0.0, pltpu.roll(x, n - 1, 1))
+    n = x.shape[1] // 128
+    turned = [pltpu.roll(x[:, 128 * c : 128 * c + 128], 127, 1) for c in range(n)]
+    edge = iota(turned[0].shape, 1) == 127
+    return jnp.concatenate([jnp.where(edge, turned[c + 1] if c < n - 1 else 0.0, turned[c]) for c in range(n)], axis=1)
 
 
 def left(x):
-    return jnp.where(iota(x.shape, 1) == 0, 0.0, pltpu.roll(x, 1, 1))
+    n = x.shape[1] // 128
+    turned = [pltpu.roll(x[:, 128 * c : 128 * c + 128], 1, 1) for c in range(n)]
+    edge = iota(turned[0].shape, 1) == 0
+    return jnp.concatenate([jnp.where(edge, turned[c - 1] if c else 0.0, turned[c]) for c in range(n)], axis=1)
 
 
 def weigh(weights, terms):
@@ -149,11 +154,8 @@
 def heat_mean(x, keep, matrix_ref):
     sums = []
     for t in windows(x, matrix_ref, True):
-        total = 0.0
-        for j in range(4):
-            for h in range(2):
-                piece = t[keep * j : keep * j + keep, 128 * h : 128 * h + 128]
-                total = total + piece * (1.0 + 0.5 * piece)
+        pieces = [t[keep * j : keep * j + keep, 128 * h : 128 * h + 128] for j in range(4) for h in range(2)]
+        total = sum(pieces[1:], pieces[0]) + 0.5 * sum((p * p for p in pieces[1:]), pieces[0] * pieces[0])
         sums.append(pltpu.roll(total, 64, 1))
     low_half = iota((keep, 128), 1) < 64
     return 0.125 * jnp.concatenate([jnp.where(low_half, sums[c], sums[c + 1]) for c in range(4)], axis=1)
@@ -259,13 +261,23 @@
     to_sides(near_ref, far_ref, 8, up, down)
 
 
-def coarse_rate(q, below, above, speeds, positives, diffusion, keep):
+def winds(speeds):
+    sizes = [DT * jnp.abs(a) for a in speeds]
+    total = sizes[0] + sizes[1] + sizes[2]
+    rests = {k: (1.0 - 6.0 * DT * k) - total for k in set(KINDS)}
+    return [a > 0 for a in speeds], sizes, rests
+
+
+def coarse_step(q, below, above, shared, diffusion, keep):
+    positives, sizes, rests = shared
     x = q[:keep]
-    up = (above - x, right(x) - x, row(q, 1)[:keep] - x)
-    down = (x - below, x - left(x), x - row(q, -1)[:keep])
-    spread = (up[0] - down[0]) + (up[1] - down[1]) + (up[2] - down[2])
-    carried = sum(upwind(a, s, d, u) for a, s, d, u in zip(speeds, positives, down, up))
-    return diffusion * spread - carried
+    after = (above, right(x), row(q, 1)[:keep])
+    before = (below, left(x), row(q, -1)[:keep])
+    around = ((after[0] + before[0]) + (after[1] + before[1])) + (after[2] + before[2])
+    total = x * rests[diffusion] + (DT * diffusion) * around
+    for positive, size, b, a in zip(positives, sizes, before, after):
+        total = total + size * jnp.where(positive, b, a)
+    return total
 
 
 def salt_step(x, below, above, before, after, speeds):
@@ -320,34 +332,36 @@
             cp[f, m + 2, 0:8, :] = c_ref[f, m]
             cp[f, m + 2, 8:16, :] = rim_of(ur_ref, dr_ref, f, m)
     own_matrix = own_ref[z]
-    for f in range(3):
-        vel[f] = refined_rows(by_levels_rows(own_matrix, cp[f, 2:6]), refine_ref)
+    heat = by_levels_rows(all_ref[...], cp[3, 2:6])
+    winding = [by_levels_rows(own_matrix, cp[f, 2:6]) for f in range(3)]
     rows16 = iota((16, NX), 0)
     inside = ((rows16 < 8) | (rows16 >= 12) | (place != 127)) & ((rows16 < 12) | (place != 0))
-    heat = by_levels_rows(all_ref[...], cp[3, 2:6])
+    two = iota((8, NX), 0) < 2
     for m in range(4):
-        own_level = z == m // 2
-        below = jnp.where(own_level, dr_ref[11], dr_ref[8])
-        above = jnp.where(own_level, ur_ref[11], ur_ref[8])
-        if m % 2 == 1:
-            below = pltpu.roll(below, 6, 0)
-            above = pltpu.roll(above, 4, 0)
-        else:
-            above = pltpu.roll(above, 6, 0)
-        rim = jnp.where(iota((8, NX), 0) < 2, below, above)
-        salt_mean = jnp.concatenate([c_ref[4, m], rim], axis=0)
-        buoyancy = heat_mean(heat[64 * m : 64 * m + 64], 16, refine_split_ref) - 0.8 * salt_mean
-        speeds = [cp[f, m + 2] for f in range(3)]
-        positives = [s > 0 for s in speeds]
-        for f in range(4):
-            q = cp[f, m + 2]
-            rate = coarse_rate(q, cp[f, m + 1], cp[f, m + 3], speeds, positives, KINDS[f], 16)
+        shared = winds([cp[f, m + 2] for f in range(3)])
+        for f in (3, 1, 2, 0):
+            mid = coarse_step(cp[f, m + 2], cp[f, m + 1], cp[f, m + 3], shared, KINDS[f], 16)
             if f == 0:
-                rate = rate + buoyancy
-            mp[f, m + 2] = jnp.where(inside, q + DT * rate, 0.0)
+                own_level = z == m // 2
+                below = jnp.where(own_level, dr_ref[11], dr_ref[8])
+                above = jnp.where(own_level, ur_ref[11], ur_ref[8])
+                if m % 2 == 1:
+                    below = pltpu.roll(below, 6, 0)
+                    above = pltpu.roll(above, 4, 0)
+                else:
+                    above = pltpu.roll(above, 6, 0)
+                salt_mean = jnp.concatenate([c_ref[4, m], jnp.where(two, below, above)], axis=0)
+                buoyancy = heat_mean(heat[64 * m : 64 * m + 64], 16, refine_split_ref) - 0.8 * salt_mean
+                mid = mid + DT * buoyancy
+            mp[f, m + 2] = jnp.where(inside, mid, 0.0)
+        if m < 3:
+            vel[m] = refined_rows(winding[m], refine_ref)
+    heat = by_levels_rows(own_matrix, mp[3, 2:6])
     line = iota((8, NF), 0)
     totals = []
+    heats = []
     for m in range(2):
+        heats.append(heat_mean(heat[32 * m : 32 * m + 32], 8, refine_split_ref))
         total = None
         for p in range(2):
             l = 2 * m + p
@@ -366,19 +380,16 @@
                 total = mid if total is None else total + mid
         totals.append(total)
     means = restrict(jnp.concatenate(totals, axis=0), restrict_ref[...])
-    heat = by_levels_rows(own_matrix, mp[3, 2:6])
     for m in range(2):
-        buoyancy = heat_mean(heat[32 * m : 32 * m + 32], 8, refine_split_ref) - 0.8 * means[8 * m : 8 * m + 8]
         at = 2 * z + m + 2
-        speeds = [mp[f, at, 0:8, :] for f in range(3)]
-        positives = [s > 0 for s in speeds]
+        shared = winds([mp[f, at, 0:8, :] for f in range(3)])
         ends = []
-        for f in range(4):
-            q = mp[f, at]
-            rate = coarse_rate(q, mp[f, at - 1, 0:8, :], mp[f, at + 1, 0:8, :], speeds, positives, KINDS[f], 8)
+        for f in (1, 2, 3, 0):
+            end = coarse_step(mp[f, at], mp[f, at - 1, 0:8, :], mp[f, at + 1, 0:8, :], shared, KINDS[f], 8)
             if f == 0:
-                rate = rate + buoyancy
-            ends.append(0.5 * cp[f, at, 0:8, :] + 0.5 * (q[:8] + DT * rate))
+                end = end + DT * (heats[m] - 0.8 * means[8 * m : 8 * m + 8])
+            ends.append(0.5 * cp[f, at, 0:8, :] + 0.5 * end)
+        ends = ends[3:] + ends[:3]
         for b in range(4):
             tiles = turn_blocks([ends[f][:, 128 * b : 128 * b + 128] for f in range(4)])
             for j in range(4):

time: 59.3 us -> 58.9 us (level)
  no operation moved by 1% of the time
where the time goes in v4:
time: 58.9 us; the launch traced here: 58.6 us
  starting transfers between devices  28.3 us (48%)
  waiting for transfers between devices  21.1 us (36%)
  Pallas kernels  7.74 us (13%)
  between operations  0.77 us (1%)
  local copies, waits for them, and re-layouts  0.67 us (1%)
    ppermute x5, waiting for transfers between devices, swap(): return lax.ppermute(x, axes, pairs)  10.6 us
    all_to_all x1, starting transfers between devices, step(): d = lax.all_to_all(a.reshape(32, 2, 8, 128), ('gy', 'gz'), 0, 0, tiled=True)  10.5 us
    ppermute x5, starting transfers between devices, swap(): return lax.ppermute(x, axes, pairs)  9.05 us
    all_to_all x1, starting transfers between devices, step(): back = lax.all_to_all(msg, 'gy', 0, 0, tiled=True)  8.75 us
    all_to_all x1, waiting for transfers between devices, step(): back = lax.all_to_all(msg, 'gy', 0, 0, tiled=True)  6.91 us
    all_to_all x1, waiting for transfers between devices, step(): d = lax.all_to_all(a.reshape(32, 2, 8, 128), ('gy', 'gz'), 0, 0, tiled=True)  3.6 us
    pallas_call x1, Pallas kernels, step(): call(coarse_kernel, 'vvvvvvvvvvvv', [(16, 2, 8, 128)] + fields + [(4, 2,...  2.54 us
    pallas_call x1, Pallas kernels, step(): call(salt_kernel, 'vvvvvvvvv', [(4, 16, NF)], [vmem((3, 64, NF), F32), vm...  2.27 us
  transfers between devices with their start and end apart: 7, of which 4 were waited for; matrix products, arithmetic and copies ran while one was open for 0% of the time, Pallas kernels for 4%

profile of v4, /device:TPU:7, one launch (start us, length us, event | category | flops | bytes accessed | tf_op | source)
XLA Modules:
  0.0 58.6 jit_solution(15836323638703229490)
XLA Ops:
  0.6 1.7 %shard_map.103 = f32[16,2,2,8,128]{4,3,2,1,0:T(8,128)} custom-call(f32[3,2,32,128]{3,2,1,0:T(8,128)} %flow_hbm.1, f32[2,32,128]{2,1,0:T(8,128)} %heat_hbm.1), custom_call_target="tpu_custom_call" | custom-call | tf_op jit(solution)/shard_map/pallas_call | solution.py:496
  2.4 0.0 copy-start.2
  2.4 0.0 copy-start.3
  2.4 10.5 %all-to-all-start = ((f32[32,2,8,128]{3,2,1,0:T(8,128)}), f32[32,2,8,128]{3,2,1,0:T(8,128)S(1)}, u32[]{:S(2)}, u32[]{:S(2)}) async-start(f32[32,2,8,128]{3,2,1,0:T(8,128)} %bitcast.3), calls=%async_computation | async-start | bytes 524288 | tf_op jit(solution)/shard_map/all_to_all | solution.py:508
  12.9 0.0 copy-done.2
  12.9 0.0 copy-done.3
  12.9 0.2 shard_map.104
  13.1 0.2 collective-permute-start
  13.3 6.8 %collective-permute-done.g_ref = f32[10,8,512]{2,1,0:T(8,128)S(1)} collective-permute-done((f32[10,8,512]{2,1,0:T(8,128)S(1)}, f32[10,8,512]{2,1,0:T(8,128)S(1)}, u32[]{:S(2)}, u32[]{:S(2)}) %collective-permute-start) | collective-permute-done | bytes 163872 | tf_op jit(solution)/shard_map/ppermute | solution.py:486
  20.2 3.6 %all-to-all-done = f32[32,2,8,128]{3,2,1,0:T(8,128)S(1)} async-done(((f32[32,2,8,128]{3,2,1,0:T(8,128)}), f32[32,2,8,128]{3,2,1,0:T(8,128)S(1)}, u32[]{:S(2)}, u32[]{:S(2)}) %all-to-all-start) | async-done | bytes 262176 | tf_op jit(solution)/shard_map/all_to_all | solution.py:508
  23.8 0.0 copy-start
  23.8 0.0 copy-start.1
  23.8 0.0 copy-start.4
  23.8 0.0 copy-start.5
  23.8 0.3 shard_map.105
  24.0 1.7 %collective-permute-start.1 = (f32[9,8,512]{2,1,0:T(8,128)S(1)}, f32[9,8,512]{2,1,0:T(8,128)S(1)}, u32[]{:S(2)}, u32[]{:S(2)}) collective-permute-start(f32[9,8,512]{2,1,0:T(8,128)S(1)} %get-tuple-element.22), channel_id=1, source_target_pairs={{0,2},{2,0},{4,6},{6,4},{8,10},{10,8},{12,14},{14,12},{16,18},{18,... | collective-permute-start | bytes 442376 | tf_op jit(solution)/shard_map/ppermute | solution.py:486
  25.7 2.1 %collective-permute-start.2 = (f32[9,8,512]{2,1,0:T(8,128)S(1)}, f32[9,8,512]{2,1,0:T(8,128)S(1)}, u32[]{:S(2)}, u32[]{:S(2)}) collective-permute-start(f32[9,8,512]{2,1,0:T(8,128)S(1)} %get-tuple-element.23), channel_id=1, source_target_pairs={{2,4},{4,2},{6,8},{8,6},{10,12},{12,10},{14,16},{16,14},{18,20},{2... | collective-permute-start | bytes 442376 | tf_op jit(solution)/shard_map/ppermute | solution.py:486
  27.8 3.2 %collective-permute-start.3 = (f32[3,8,512]{2,1,0:T(8,128)S(1)}, f32[3,8,512]{2,1,0:T(8,128)S(1)}, u32[]{:S(2)}, u32[]{:S(2)}) collective-permute-start(f32[3,8,512]{2,1,0:T(8,128)S(1)} %get-tuple-element.24), channel_id=1, source_target_pairs={{0,2},{2,0},{4,6},{6,4},{8,10},{10,8},{12,14},{14,12},{16,18},{18,... | collective-permute-start | bytes 147464 | tf_op jit(solution)/shard_map/ppermute | solution.py:486
  31.0 1.9 %collective-permute-start.4 = (f32[3,8,512]{2,1,0:T(8,128)S(1)}, f32[3,8,512]{2,1,0:T(8,128)S(1)}, u32[]{:S(2)}, u32[]{:S(2)}) collective-permute-start(f32[3,8,512]{2,1,0:T(8,128)S(1)} %get-tuple-element.25), channel_id=1, source_target_pairs={{2,4},{4,2},{6,8},{8,6},{10,12},{12,10},{14,16},{16,14},{18,20},{2... | collective-permute-start | bytes 147464 | tf_op jit(solution)/shard_map/ppermute | solution.py:486
  32.9 0.0 collective-permute-done.3.near_salt_ref
  32.9 3.8 %collective-permute-done.4.far_salt_ref = f32[3,8,512]{2,1,0:T(8,128)S(1)} collective-permute-done((f32[3,8,512]{2,1,0:T(8,128)S(1)}, f32[3,8,512]{2,1,0:T(8,128)S(1)}, u32[]{:S(2)}, u32[]{:S(2)}) %collective-permute-start.4) | collective-permute-done | bytes 49184 | tf_op jit(solution)/shard_map/ppermute | solution.py:486
  36.7 0.0 collective-permute-done.1.near_ref
  36.7 0.0 collective-permute-done.2.far_ref
  36.7 0.0 copy-done
  36.7 0.0 copy-done.1
  36.7 0.0 copy-done.4
  36.7 0.0 copy-done.5
  36.7 2.5 %shard_map.106 = (f32[16,2,8,128]{3,2,1,0:T(8,128)S(1)}, f32[4,8,16,512]{3,2,1,0:T(8,128)S(1)}, f32[4,8,16,512]{3,2,1,0:T(8,128)S(1)}, f32[4,2,8,1024]{3,2,1,0:T...) custom-call(f32[5,4,8,512]{3,2,1,0:T(8,128)S(1)} %get-tuple-element.21.c_ref, ...), custom_call_target="tpu_custom_call" | custom-call | tf_op jit(solution)/shard_map/pallas_call | solution.py:514
  39.3 0.0 copy-start.6
  39.3 0.6 %copy-done.6 = f32[16,2,8,128]{3,2,1,0:T(8,128)} copy-done((f32[16,2,8,128]{3,2,1,0:T(8,128)}, f32[16,2,8,128]{3,2,1,0:T(8,128)S(1)}, u32[]{:S(2)}) %copy-start.6) | copy-done | bytes 131096
  39.9 8.7 %all-to-all-start.1 = ((f32[16,2,8,128]{3,2,1,0:T(8,128)}), f32[16,2,8,128]{3,2,1,0:T(8,128)S(1)}, u32[]{:S(2)}, u32[]{:S(2)}) async-start(f32[16,2,8,128]{3,2,1,0:T(8,128)} %copy-done.6), calls=%async_computation.1 | async-start | bytes 262144 | tf_op jit(solution)/shard_map/all_to_all | solution.py:517
  48.7 2.3 %shard_map.108 = f32[4,16,1024]{2,1,0:T(8,128)} custom-call(f32[4,8,16,512]{3,2,1,0:T(8,128)S(1)} %get-tuple-element.30.cp, f32[4,8,16,512]{3,2,1,0:T(8,128)S(1)} %get-tuple-element.31.mv, f32[4,2,8,1024]{3,2,1,0:T(8,128)S(1)} %get-tuple-element.32.salt_mid_ref, f32[4,2,8,1024]{3,2,1,0:T(8,128)S(1)} %get-tuple-element.26.plane_ref, ...), custom_call_target="tpu_custom_call" | custom-call | tf_op jit(solution)/shard_map/pallas_call | solution.py:518
  51.0 6.9 %all-to-all-done.1.x_ref = f32[16,2,8,128]{3,2,1,0:T(8,128)S(1)} async-done(((f32[16,2,8,128]{3,2,1,0:T(8,128)}), f32[16,2,8,128]{3,2,1,0:T(8,128)S(1)}, u32[]{:S(2)}, u32[]{:S(2)}) %all-to-all-start.1) | async-done | bytes 131104 | tf_op jit(solution)/shard_map/all_to_all | solution.py:517
  57.9 0.7 %shard_map.107 = (f32[3,2,32,128]{3,2,1,0:T(8,128)}, f32[2,32,128]{2,1,0:T(8,128)}) custom-call(f32[16,2,8,128]{3,2,1,0:T(8,128)S(1)} %all-to-all-done.1.x_ref), custom_call_target="tpu_custom_call" | custom-call | tf_op jit(solution)/shard_map/pallas_call | solution.py:524
Async XLA Ops:
  2.4 10.5 %copy-start.2 = (bf16[256,128]{1,0:T(8,128)(2,1)S(1)}, bf16[256,128]{1,0:T(8,128)(2,1)}, u32[]{:S(2)}) copy-start(bf16[256,128]{1,0:T(8,128)(2,1)} %constant.12.clone.restrict_ref) | copy-start | bytes 196612
  2.4 10.5 %copy-start.3 = (f32[4,16,1024]{2,1,0:T(8,128)S(1)}, f32[4,16,1024]{2,1,0:T(8,128)}, u32[]{:S(2)}) copy-start(f32[4,16,1024]{2,1,0:T(8,128)} %salt_ref.1) | copy-start | bytes 786436
  2.4 21.4 %all-to-all-start = ((f32[32,2,8,128]{3,2,1,0:T(8,128)}), f32[32,2,8,128]{3,2,1,0:T(8,128)S(1)}, u32[]{:S(2)}, u32[]{:S(2)}) async-start(f32[32,2,8,128]{3,2,1,0:T(8,128)} %bitcast.3), calls=%async_computation | async-start | bytes 524288 | tf_op jit(solution)/shard_map/all_to_all | solution.py:508
  13.1 7.0 %collective-permute-start = (f32[10,8,512]{2,1,0:T(8,128)S(1)}, f32[10,8,512]{2,1,0:T(8,128)S(1)}, u32[]{:S(2)}, u32[]{:S(2)}) collective-permute-start(f32[10,8,512]{2,1,0:T(8,128)S(1)} %get-tuple-element.20), channel_id=1, source_target_pairs={{0,1},{1,0},{2,3},{3,2},{4,5},{5,4},{6,7},{7,6},{8,9},{9,8},{10,11... | collective-permute-start | bytes 491528 | tf_op jit(solution)/shard_map/ppermute | solution.py:486
  23.8 12.9 %copy-start = (bf16[256,256]{1,0:T(8,128)(2,1)S(1)}, bf16[256,256]{1,0:T(8,128)(2,1)}, u32[]{:S(2)}) copy-start(bf16[256,256]{1,0:T(8,128)(2,1)} %constant.10.clone.refine_ref) | copy-start | bytes 393220
  23.8 12.9 %copy-start.1 = (bf16[2,64,192]{2,1,0:T(8,128)(2,1)S(1)}, bf16[2,64,192]{2,1,0:T(8,128)(2,1)}, u32[]{:S(2)}) copy-start(bf16[2,64,192]{2,1,0:T(8,128)(2,1)} %constant.13.clone.own_ref) | copy-start | bytes 147460
  23.8 12.9 %copy-start.4 = (bf16[256,192]{1,0:T(8,128)(2,1)S(1)}, bf16[256,192]{1,0:T(8,128)(2,1)}, u32[]{:S(2)}) copy-start(bf16[256,192]{1,0:T(8,128)(2,1)} %constant.14.clone.all_ref) | copy-start | bytes 294916
  23.8 13.0 %copy-start.5 = (bf16[256,256]{1,0:T(8,128)(2,1)S(1)}, bf16[256,256]{1,0:T(8,128)(2,1)}, u32[]{:S(2)}) copy-start(bf16[256,256]{1,0:T(8,128)(2,1)} %constant.11.clone.refine_split_ref) | copy-start | bytes 393220
  24.0 12.6 %collective-permute-start.1 = (f32[9,8,512]{2,1,0:T(8,128)S(1)}, f32[9,8,512]{2,1,0:T(8,128)S(1)}, u32[]{:S(2)}, u32[]{:S(2)}) collective-permute-start(f32[9,8,512]{2,1,0:T(8,128)S(1)} %get-tuple-element.22), channel_id=1, source_target_pairs={{0,2},{2,0},{4,6},{6,4},{8,10},{10,8},{12,14},{14,12},{16,18},{18,... | collective-permute-start | bytes 442376 | tf_op jit(solution)/shard_map/ppermute | solution.py:486
  25.7 11.0 %collective-permute-start.2 = (f32[9,8,512]{2,1,0:T(8,128)S(1)}, f32[9,8,512]{2,1,0:T(8,128)S(1)}, u32[]{:S(2)}, u32[]{:S(2)}) collective-permute-start(f32[9,8,512]{2,1,0:T(8,128)S(1)} %get-tuple-element.23), channel_id=1, source_target_pairs={{2,4},{4,2},{6,8},{8,6},{10,12},{12,10},{14,16},{16,14},{18,20},{2... | collective-permute-start | bytes 442376 | tf_op jit(solution)/shard_map/ppermute | solution.py:486
  27.8 5.1 %collective-permute-start.3 = (f32[3,8,512]{2,1,0:T(8,128)S(1)}, f32[3,8,512]{2,1,0:T(8,128)S(1)}, u32[]{:S(2)}, u32[]{:S(2)}) collective-permute-start(f32[3,8,512]{2,1,0:T(8,128)S(1)} %get-tuple-element.24), channel_id=1, source_target_pairs={{0,2},{2,0},{4,6},{6,4},{8,10},{10,8},{12,14},{14,12},{16,18},{18,... | collective-permute-start | bytes 147464 | tf_op jit(solution)/shard_map/ppermute | solution.py:486
  31.0 5.7 %collective-permute-start.4 = (f32[3,8,512]{2,1,0:T(8,128)S(1)}, f32[3,8,512]{2,1,0:T(8,128)S(1)}, u32[]{:S(2)}, u32[]{:S(2)}) collective-permute-start(f32[3,8,512]{2,1,0:T(8,128)S(1)} %get-tuple-element.25), channel_id=1, source_target_pairs={{2,4},{4,2},{6,8},{8,6},{10,12},{12,10},{14,16},{16,14},{18,20},{2... | collective-permute-start | bytes 147464 | tf_op jit(solution)/shard_map/ppermute | solution.py:486
  39.3 0.7 %copy-start.6 = (f32[16,2,8,128]{3,2,1,0:T(8,128)}, f32[16,2,8,128]{3,2,1,0:T(8,128)S(1)}, u32[]{:S(2)}) copy-start(f32[16,2,8,128]{3,2,1,0:T(8,128)S(1)} %get-tuple-element.27) | copy-start | bytes 393220
  39.9 17.9 %all-to-all-start.1 = ((f32[16,2,8,128]{3,2,1,0:T(8,128)}), f32[16,2,8,128]{3,2,1,0:T(8,128)S(1)}, u32[]{:S(2)}, u32[]{:S(2)}) async-start(f32[16,2,8,128]{3,2,1,0:T(8,128)} %copy-done.6), calls=%async_computation.1 | async-start | bytes 262144 | tf_op jit(solution)/shard_map/all_to_all | solution.py:517

commit v5 on v4

--- a/solution.py
+++ b/solution.py
@@ -237,8 +237,18 @@
     return jnp.where(z == m // 2, mean_ref[m % 2], g_ref[8 + m % 2])
 
 
-def send_kernel(d_ref, mean_ref, g_ref, c_ref, near_ref, far_ref):
+def other_rows(g_ref, last):
+    low, high = (g_ref[8], g_ref[9])
+    if last:
+        rows = [jnp.broadcast_to(g_ref[2 + h, 7:8, :], (8, NX)) for h in range(2)]
+        return few_rows(pltpu.roll(low, 2, 0), pltpu.roll(high, 2, 0), rows[0], rows[1])
+    rows = [jnp.broadcast_to(g_ref[h, 0:1, :], (8, NX)) for h in range(2)]
+    return few_rows(low, high, rows[0], rows[1])
+
+
+def send_kernel(d_ref, mean_ref, g_ref, own_ref, c_ref, near_ref, far_ref):
     z = lax.axis_index("gz")
+    place = lax.axis_index("gx") * 16 + lax.axis_index("gy")
     for m in range(4):
         for b in range(4):
             tiles = turn_blocks([d_ref[4 * b + j, m] for j in range(4)])
@@ -253,12 +263,11 @@
             down = jnp.where(first, a, pltpu.roll(b, 4, 0))
             up = jnp.where(first, pltpu.roll(a, 4, 0), b)
             to_sides(near_ref, far_ref, 2 * f + p, up, down)
-    low, high = (g_ref[8], g_ref[9])
-    rows = [jnp.broadcast_to(g_ref[h, 0:1, :], (8, NX)) for h in range(2)]
-    down = few_rows(low, high, rows[0], rows[1])
-    rows = [jnp.broadcast_to(g_ref[2 + h, 7:8, :], (8, NX)) for h in range(2)]
-    up = few_rows(pltpu.roll(low, 2, 0), pltpu.roll(high, 2, 0), rows[0], rows[1])
+    up, down = other_rows(g_ref, True), other_rows(g_ref, False)
     to_sides(near_ref, far_ref, 8, up, down)
+    crossing = (place == 63) | (place == 64)
+    own = jnp.where(place == 63, other_rows(own_ref, True), other_rows(own_ref, False))
+    far_ref[8] = jnp.where(crossing, own, far_ref[8])
 
 
 def winds(speeds):
@@ -486,6 +495,15 @@
     return lax.ppermute(x, axes, pairs)
 
 
+def beside(crossing):
+    pairs = []
+    for r in range(1, 127, 2):
+        for z in range(2):
+            other = 1 - z if r in crossing else z
+            pairs += [(2 * r + z, 2 * r + 2 + other), (2 * r + 2 + other, 2 * r + z)]
+    return pairs
+
+
 def step(flow, heat, salt):
     vmem = pltpu.VMEM
     refine = jnp.asarray(REFINE, BF16)
@@ -502,13 +520,16 @@
         [(10, 8, NX), (2, 8, NX), (4, 2, 8, NF), (3, 8, NX), (3, 8, NX)],
         [vmem((8, 4, 16, 128), F32), vmem((2, 8, NX), F32), vmem((2, 8, NX), F32)],
     )(salt, restrict_m)
+    own = g
     g = swap(g, "gz", 2, 0)
     near_salt = swap(near_salt, ("gx", "gy"), 128, 0)
     far_salt = swap(far_salt, ("gx", "gy"), 128, 1)
     d = lax.all_to_all(a.reshape(32, 2, 8, 128), ("gy", "gz"), 0, 0, tiled=True)
-    c, near, far = call(send_kernel, "vvv", [(5, 4, 8, NX), (9, 8, NX), (9, 8, NX)])(d.reshape(16, 4, 8, 128), means, g)
+    c, near, far = call(send_kernel, "vvvv", [(5, 4, 8, NX), (9, 8, NX), (9, 8, NX)])(
+        d.reshape(16, 4, 8, 128), means, g, own
+    )
     near = swap(near, ("gx", "gy"), 128, 0)
-    far = swap(far, ("gx", "gy"), 128, 1)
+    far = lax.ppermute(far, ("gx", "gy", "gz"), beside((63,)))
     rims = [(12, 8, NX)] * 2
     fields = [(4, 8, 16, NX)] * 2
     msg, cp, mp, salt_mid, u, v = call(

time: 58.9 us -> 58.2 us (0.988)
  starting transfers between devices: 28.3 us -> 27.5 us
    ppermute x5 -> x4, starting transfers between devices: 9.05 us -> 6.09 us  [swap(): return lax.ppermute(x, axes, pairs)]
    ppermute x0 -> x1, starting transfers between devices: none -> 2.12 us  [step(): far = lax.ppermute(far, ('gx', 'gy', 'gz'), beside((63,)))]
    ppermute x5 -> x4, waiting for transfers between devices: 10.6 us -> 10.6 us  [swap(): return lax.ppermute(x, axes, pairs)]
where the time goes in v5:
time: 58.2 us; the launch traced here: 57.8 us
  starting transfers between devices  27.5 us (47%)
  waiting for transfers between devices  21.1 us (36%)
  Pallas kernels  7.74 us (13%)
  between operations  0.77 us (1%)
  local copies, waits for them, and re-layouts  0.67 us (1%)
    ppermute x4, waiting for transfers between devices, swap(): return lax.ppermute(x, axes, pairs)  10.6 us
    all_to_all x1, starting transfers between devices, step(): d = lax.all_to_all(a.reshape(32, 2, 8, 128), ('gy', 'gz'), 0, 0, tiled=True)  10.5 us
    all_to_all x1, starting transfers between devices, step(): back = lax.all_to_all(msg, 'gy', 0, 0, tiled=True)  8.75 us
    all_to_all x1, waiting for transfers between devices, step(): back = lax.all_to_all(msg, 'gy', 0, 0, tiled=True)  6.91 us
    ppermute x4, starting transfers between devices, swap(): return lax.ppermute(x, axes, pairs)  6.09 us
    all_to_all x1, waiting for transfers between devices, step(): d = lax.all_to_all(a.reshape(32, 2, 8, 128), ('gy', 'gz'), 0, 0, tiled=True)  3.6 us
    pallas_call x1, Pallas kernels, step(): call(coarse_kernel, 'vvvvvvvvvvvv', [(16, 2, 8, 128)] + fields + [(4, 2,...  2.54 us
    pallas_call x1, Pallas kernels, step(): call(salt_kernel, 'vvvvvvvvv', [(4, 16, NF)], [vmem((3, 64, NF), F32), vm...  2.27 us
  transfers between devices with their start and end apart: 7, of which 4 were waited for; matrix products, arithmetic and copies ran while one was open for 0% of the time, Pallas kernels for 4%

profile of v5, /device:TPU:7, one launch (start us, length us, event | category | flops | bytes accessed | tf_op | source)
XLA Modules:
  0.0 57.8 jit_solution(8402112284865004972)
XLA Ops:
  0.6 1.7 %shard_map.103 = f32[16,2,2,8,128]{4,3,2,1,0:T(8,128)} custom-call(f32[3,2,32,128]{3,2,1,0:T(8,128)} %flow_hbm.1, f32[2,32,128]{2,1,0:T(8,128)} %heat_hbm.1), custom_call_target="tpu_custom_call" | custom-call | tf_op jit(solution)/shard_map/pallas_call | solution.py:514
  2.4 0.0 copy-start.2
  2.4 0.0 copy-start.3
  2.4 10.5 %all-to-all-start = ((f32[32,2,8,128]{3,2,1,0:T(8,128)}), f32[32,2,8,128]{3,2,1,0:T(8,128)S(1)}, u32[]{:S(2)}, u32[]{:S(2)}) async-start(f32[32,2,8,128]{3,2,1,0:T(8,128)} %bitcast.3), calls=%async_computation | async-start | bytes 524288 | tf_op jit(solution)/shard_map/all_to_all | solution.py:527
  12.9 0.0 copy-done.2
  12.9 0.0 copy-done.3
  12.9 0.2 shard_map.104
  13.1 0.2 collective-permute-start
  13.3 6.8 %collective-permute-done.g_ref = f32[10,8,512]{2,1,0:T(8,128)S(1)} collective-permute-done((f32[10,8,512]{2,1,0:T(8,128)S(1)}, f32[10,8,512]{2,1,0:T(8,128)S(1)}, u32[]{:S(2)}, u32[]{:S(2)}) %collective-permute-start) | collective-permute-done | bytes 163872 | tf_op jit(solution)/shard_map/ppermute | solution.py:495
  20.2 3.6 %all-to-all-done = f32[32,2,8,128]{3,2,1,0:T(8,128)S(1)} async-done(((f32[32,2,8,128]{3,2,1,0:T(8,128)}), f32[32,2,8,128]{3,2,1,0:T(8,128)S(1)}, u32[]{:S(2)}, u32[]{:S(2)}) %all-to-all-start) | async-done | bytes 262176 | tf_op jit(solution)/shard_map/all_to_all | solution.py:527
  23.8 0.0 copy-start
  23.8 0.0 copy-start.1
  23.8 0.0 copy-start.4
  23.8 0.0 copy-start.5
  23.8 0.3 shard_map.105
  24.0 1.7 %collective-permute-start.1 = (f32[9,8,512]{2,1,0:T(8,128)S(1)}, f32[9,8,512]{2,1,0:T(8,128)S(1)}, u32[]{:S(2)}, u32[]{:S(2)}) collective-permute-start(f32[9,8,512]{2,1,0:T(8,128)S(1)} %get-tuple-element.22), channel_id=1, source_target_pairs={{0,2},{2,0},{4,6},{6,4},{8,10},{10,8},{12,14},{14,12},{16,18},{18,... | collective-permute-start | bytes 442376 | tf_op jit(solution)/shard_map/ppermute | solution.py:495
  25.7 2.1 %collective-permute-start.2 = (f32[9,8,512]{2,1,0:T(8,128)S(1)}, f32[9,8,512]{2,1,0:T(8,128)S(1)}, u32[]{:S(2)}, u32[]{:S(2)}) collective-permute-start(f32[9,8,512]{2,1,0:T(8,128)S(1)} %get-tuple-element.23), channel_id=1, source_target_pairs={{2,4},{4,2},{3,5},{5,3},{6,8},{8,6},{7,9},{9,7},{10,12},{12,10},{1... | collective-permute-start | bytes 442376 | tf_op jit(solution)/shard_map/ppermute | solution.py:532
  27.8 2.3 %collective-permute-start.3 = (f32[3,8,512]{2,1,0:T(8,128)S(1)}, f32[3,8,512]{2,1,0:T(8,128)S(1)}, u32[]{:S(2)}, u32[]{:S(2)}) collective-permute-start(f32[3,8,512]{2,1,0:T(8,128)S(1)} %get-tuple-element.24), channel_id=1, source_target_pairs={{0,2},{2,0},{4,6},{6,4},{8,10},{10,8},{12,14},{14,12},{16,18},{18,... | collective-permute-start | bytes 147464 | tf_op jit(solution)/shard_map/ppermute | solution.py:495
  30.2 1.9 %collective-permute-start.4 = (f32[3,8,512]{2,1,0:T(8,128)S(1)}, f32[3,8,512]{2,1,0:T(8,128)S(1)}, u32[]{:S(2)}, u32[]{:S(2)}) collective-permute-start(f32[3,8,512]{2,1,0:T(8,128)S(1)} %get-tuple-element.25), channel_id=1, source_target_pairs={{2,4},{4,2},{6,8},{8,6},{10,12},{12,10},{14,16},{16,14},{18,20},{2... | collective-permute-start | bytes 147464 | tf_op jit(solution)/shard_map/ppermute | solution.py:495
  32.1 0.0 collective-permute-done.3.near_salt_ref
  32.1 3.8 %collective-permute-done.4.far_salt_ref = f32[3,8,512]{2,1,0:T(8,128)S(1)} collective-permute-done((f32[3,8,512]{2,1,0:T(8,128)S(1)}, f32[3,8,512]{2,1,0:T(8,128)S(1)}, u32[]{:S(2)}, u32[]{:S(2)}) %collective-permute-start.4) | collective-permute-done | bytes 49184 | tf_op jit(solution)/shard_map/ppermute | solution.py:495
  35.9 0.0 collective-permute-done.1.near_ref
  35.9 0.0 collective-permute-done.2.far_ref
  35.9 0.0 copy-done
  35.9 0.0 copy-done.1
  35.9 0.0 copy-done.4
  35.9 0.0 copy-done.5
  35.9 2.5 %shard_map.106 = (f32[16,2,8,128]{3,2,1,0:T(8,128)S(1)}, f32[4,8,16,512]{3,2,1,0:T(8,128)S(1)}, f32[4,8,16,512]{3,2,1,0:T(8,128)S(1)}, f32[4,2,8,1024]{3,2,1,0:T...) custom-call(f32[5,4,8,512]{3,2,1,0:T(8,128)S(1)} %get-tuple-element.21.c_ref, ...), custom_call_target="tpu_custom_call" | custom-call | tf_op jit(solution)/shard_map/pallas_call | solution.py:535
  38.4 0.0 copy-start.6
  38.4 0.6 %copy-done.6 = f32[16,2,8,128]{3,2,1,0:T(8,128)} copy-done((f32[16,2,8,128]{3,2,1,0:T(8,128)}, f32[16,2,8,128]{3,2,1,0:T(8,128)S(1)}, u32[]{:S(2)}) %copy-start.6) | copy-done | bytes 131096
  39.1 8.8 %all-to-all-start.1 = ((f32[16,2,8,128]{3,2,1,0:T(8,128)}), f32[16,2,8,128]{3,2,1,0:T(8,128)S(1)}, u32[]{:S(2)}, u32[]{:S(2)}) async-start(f32[16,2,8,128]{3,2,1,0:T(8,128)} %copy-done.6), calls=%async_computation.1 | async-start | bytes 262144 | tf_op jit(solution)/shard_map/all_to_all | solution.py:538
  47.8 2.3 %shard_map.108 = f32[4,16,1024]{2,1,0:T(8,128)} custom-call(f32[4,8,16,512]{3,2,1,0:T(8,128)S(1)} %get-tuple-element.30.cp, f32[4,8,16,512]{3,2,1,0:T(8,128)S(1)} %get-tuple-element.31.mv, f32[4,2,8,1024]{3,2,1,0:T(8,128)S(1)} %get-tuple-element.32.salt_mid_ref, f32[4,2,8,1024]{3,2,1,0:T(8,128)S(1)} %get-tuple-element.26.plane_ref, ...), custom_call_target="tpu_custom_call" | custom-call | tf_op jit(solution)/shard_map/pallas_call | solution.py:539
  50.1 6.9 %all-to-all-done.1.x_ref = f32[16,2,8,128]{3,2,1,0:T(8,128)S(1)} async-done(((f32[16,2,8,128]{3,2,1,0:T(8,128)}), f32[16,2,8,128]{3,2,1,0:T(8,128)S(1)}, u32[]{:S(2)}, u32[]{:S(2)}) %all-to-all-start.1) | async-done | bytes 131104 | tf_op jit(solution)/shard_map/all_to_all | solution.py:538
  57.0 0.7 %shard_map.107 = (f32[3,2,32,128]{3,2,1,0:T(8,128)}, f32[2,32,128]{2,1,0:T(8,128)}) custom-call(f32[16,2,8,128]{3,2,1,0:T(8,128)S(1)} %all-to-all-done.1.x_ref), custom_call_target="tpu_custom_call" | custom-call | tf_op jit(solution)/shard_map/pallas_call | solution.py:545
Async XLA Ops:
  2.4 10.5 %copy-start.2 = (bf16[256,128]{1,0:T(8,128)(2,1)S(1)}, bf16[256,128]{1,0:T(8,128)(2,1)}, u32[]{:S(2)}) copy-start(bf16[256,128]{1,0:T(8,128)(2,1)} %constant.12.clone.restrict_ref) | copy-start | bytes 196612
  2.4 10.5 %copy-start.3 = (f32[4,16,1024]{2,1,0:T(8,128)S(1)}, f32[4,16,1024]{2,1,0:T(8,128)}, u32[]{:S(2)}) copy-start(f32[4,16,1024]{2,1,0:T(8,128)} %salt_ref.1) | copy-start | bytes 786436
  2.4 21.4 %all-to-all-start = ((f32[32,2,8,128]{3,2,1,0:T(8,128)}), f32[32,2,8,128]{3,2,1,0:T(8,128)S(1)}, u32[]{:S(2)}, u32[]{:S(2)}) async-start(f32[32,2,8,128]{3,2,1,0:T(8,128)} %bitcast.3), calls=%async_computation | async-start | bytes 524288 | tf_op jit(solution)/shard_map/all_to_all | solution.py:527
  13.1 7.0 %collective-permute-start = (f32[10,8,512]{2,1,0:T(8,128)S(1)}, f32[10,8,512]{2,1,0:T(8,128)S(1)}, u32[]{:S(2)}, u32[]{:S(2)}) collective-permute-start(f32[10,8,512]{2,1,0:T(8,128)S(1)} %get-tuple-element.20.own_ref), channel_id=1, source_target_pairs={{0,1},{1,0},{2,3},{3,2},{4,5},{5,4},{6,7},{7,6},{8,9},{9,8},{10,11... | collective-permute-start | bytes 491528 | tf_op jit(solution)/shard_map/ppermute | solution.py:495
  23.8 12.1 %copy-start = (bf16[256,256]{1,0:T(8,128)(2,1)S(1)}, bf16[256,256]{1,0:T(8,128)(2,1)}, u32[]{:S(2)}) copy-start(bf16[256,256]{1,0:T(8,128)(2,1)} %constant.10.clone.refine_ref) | copy-start | bytes 393220
  23.8 12.1 %copy-start.1 = (bf16[2,64,192]{2,1,0:T(8,128)(2,1)S(1)}, bf16[2,64,192]{2,1,0:T(8,128)(2,1)}, u32[]{:S(2)}) copy-start(bf16[2,64,192]{2,1,0:T(8,128)(2,1)} %constant.13.clone.own_ref) | copy-start | bytes 147460
  23.8 12.1 %copy-start.4 = (bf16[256,192]{1,0:T(8,128)(2,1)S(1)}, bf16[256,192]{1,0:T(8,128)(2,1)}, u32[]{:S(2)}) copy-start(bf16[256,192]{1,0:T(8,128)(2,1)} %constant.14.clone.all_ref) | copy-start | bytes 294916
  23.8 12.1 %copy-start.5 = (bf16[256,256]{1,0:T(8,128)(2,1)S(1)}, bf16[256,256]{1,0:T(8,128)(2,1)}, u32[]{:S(2)}) copy-start(bf16[256,256]{1,0:T(8,128)(2,1)} %constant.11.clone.refine_split_ref) | copy-start | bytes 393220
  24.0 11.8 %collective-permute-start.1 = (f32[9,8,512]{2,1,0:T(8,128)S(1)}, f32[9,8,512]{2,1,0:T(8,128)S(1)}, u32[]{:S(2)}, u32[]{:S(2)}) collective-permute-start(f32[9,8,512]{2,1,0:T(8,128)S(1)} %get-tuple-element.22), channel_id=1, source_target_pairs={{0,2},{2,0},{4,6},{6,4},{8,10},{10,8},{12,14},{14,12},{16,18},{18,... | collective-permute-start | bytes 442376 | tf_op jit(solution)/shard_map/ppermute | solution.py:495
  25.7 10.1 %collective-permute-start.2 = (f32[9,8,512]{2,1,0:T(8,128)S(1)}, f32[9,8,512]{2,1,0:T(8,128)S(1)}, u32[]{:S(2)}, u32[]{:S(2)}) collective-permute-start(f32[9,8,512]{2,1,0:T(8,128)S(1)} %get-tuple-element.23), channel_id=1, source_target_pairs={{2,4},{4,2},{3,5},{5,3},{6,8},{8,6},{7,9},{9,7},{10,12},{12,10},{1... | collective-permute-start | bytes 442376 | tf_op jit(solution)/shard_map/ppermute | solution.py:532
  27.8 4.2 %collective-permute-start.3 = (f32[3,8,512]{2,1,0:T(8,128)S(1)}, f32[3,8,512]{2,1,0:T(8,128)S(1)}, u32[]{:S(2)}, u32[]{:S(2)}) collective-permute-start(f32[3,8,512]{2,1,0:T(8,128)S(1)} %get-tuple-element.24), channel_id=1, source_target_pairs={{0,2},{2,0},{4,6},{6,4},{8,10},{10,8},{12,14},{14,12},{16,18},{18,... | collective-permute-start | bytes 147464 | tf_op jit(solution)/shard_map/ppermute | solution.py:495
  30.2 5.7 %collective-permute-start.4 = (f32[3,8,512]{2,1,0:T(8,128)S(1)}, f32[3,8,512]{2,1,0:T(8,128)S(1)}, u32[]{:S(2)}, u32[]{:S(2)}) collective-permute-start(f32[3,8,512]{2,1,0:T(8,128)S(1)} %get-tuple-element.25), channel_id=1, source_target_pairs={{2,4},{4,2},{6,8},{8,6},{10,12},{12,10},{14,16},{16,14},{18,20},{2... | collective-permute-start | bytes 147464 | tf_op jit(solution)/shard_map/ppermute | solution.py:495
  38.4 0.7 %copy-start.6 = (f32[16,2,8,128]{3,2,1,0:T(8,128)}, f32[16,2,8,128]{3,2,1,0:T(8,128)S(1)}, u32[]{:S(2)}) copy-start(f32[16,2,8,128]{3,2,1,0:T(8,128)S(1)} %get-tuple-element.27) | copy-start | bytes 393220
  39.1 17.9 %all-to-all-start.1 = ((f32[16,2,8,128]{3,2,1,0:T(8,128)}), f32[16,2,8,128]{3,2,1,0:T(8,128)S(1)}, u32[]{:S(2)}, u32[]{:S(2)}) async-start(f32[16,2,8,128]{3,2,1,0:T(8,128)} %copy-done.6), calls=%async_computation.1 | async-start | bytes 262144 | tf_op jit(solution)/shard_map/all_to_all | solution.py:538
